TPU v7x, 512 devices: a whole 4x4x16 slice. The times are simulated.
512 devices in a mesh: freq: 16 (over y_hi, x, core), tm: 32 (over y_lo, z).
Axes of the slice: x: 4, y: 4 (y_hi: 2, y_lo: 2; y = y_hi * 2 + y_lo), z: 16, core: 2. Of those that a mesh axis runs over, the one named last changes fastest.
Arguments:
- signal: bfloat16 [8192, 4096], P('tm', 'freq'), may hold values from -48 to 48
- conv_first: bfloat16 [64, 9, 64, 64], P('freq'), may hold values from -0.25 to 0.25
- conv_second: bfloat16 [64, 9, 64, 64], P('freq'), may hold values from -0.25 to 0.25
- shuffle: int32 [64], replicated, may hold values from 0 to 63, each once
- blocks: int32 [8192], P('tm'), may hold values from 0 to 255, never falling along the last dimension, each value on 1 to 64 neighbouring positions
- query_weight: bfloat16 [16, 256, 128], P('freq'), may hold values from -0.25 to 0.25
- key_weight: bfloat16 [16, 256, 128], P('freq'), may hold values from -0.375 to 0.375
- value_weight: bfloat16 [16, 256, 128], P('freq'), may hold values from -0.375 to 0.375
- out_weight: bfloat16 [16, 128, 256], P('freq'), may hold values from -1.796875 to 1.796875
Outputs:
- encoded: bfloat16 [8192, 4096], P('tm', 'freq')
All inputs are finite; a program needn't handle non-finite values.
Results may differ from a plain program's by a relative error of at most 0.019.
The roundings to bfloat16 on the way count: a program that leaves them out, or rounds other values in their place, can miss the bound.
Values may be sent and summed in bfloat16 or wider, within the bound.
No kernel may reach another device: no remote copies, remote signals or barrier semaphores. Data moves between devices by JAX's collectives and lax.ppermute only.
A program may use at most 128 MiB of HBM per device.

v0:
```python
import functools
import math

import jax
import jax.numpy as jnp
from jax import lax
from jax.experimental import pallas as pl
from jax.experimental.pallas import tpu as pltpu
from jax.sharding import PartitionSpec as P

F32 = jnp.float32
BF16 = jnp.bfloat16
NEG = -1e30
FLOOR = -1e28
EXTRA = 16


def dot(a, b):
    return lax.dot_general(a, b, (((1,), (0,)), ((), ())), preferred_element_type=F32)


def dot_nt(a, b):
    return lax.dot_general(a, b, (((1,), (1,)), ((), ())), preferred_element_type=F32)


def dot_tn(a, b):
    return lax.dot_general(a, b, (((0,), (0,)), ((), ())), preferred_element_type=F32)


def iota(shape, dim):
    return lax.broadcasted_iota(jnp.int32, shape, dim)


def row_to_column(row):
    size = row.shape[1]
    square = (size, size)
    kept = jnp.where(iota(square, 0) == iota(square, 1), row, jnp.zeros_like(row))
    return jnp.sum(kept, axis=1, keepdims=True)


def column_to_row(column):
    size = column.shape[0]
    square = (size, size)
    kept = jnp.where(iota(square, 0) == iota(square, 1), column, jnp.zeros_like(column))
    return jnp.sum(kept, axis=0, keepdims=True)


def fill_diagonal(weights, wide):
    groups, taps, rows, columns = weights.shape
    width = groups * rows
    wide[...] = jnp.zeros_like(wide)
    for tap in range(taps):
        for group in range(groups):
            top = tap * width + group * rows
            wide[top : top + rows, group * columns : (group + 1) * columns] = weights[group, tap]


def fill_taps(source, taps, count, spread):
    width = source.shape[1]
    for tap in range(taps):
        start = taps - 1 - tap
        spread[:, tap * width : (tap + 1) * width] = source[start : start + count, :].astype(BF16)


def first_kernel(signal, before, weights, shuffle, out, source, spread, wide):
    groups, taps, size, _ = weights.shape
    count, width = signal.shape
    margin = taps - 1
    source[: 2 * margin, :] = before[...].astype(F32)
    source[2 * margin :, :] = signal[...].astype(F32)
    fill_diagonal(weights, wide)
    fill_taps(source, taps, count + margin, spread)
    total = dot(spread[...], wide[...])
    first = (total / (1.0 + jnp.exp(-total))).astype(BF16)
    mark = (width, size)
    chosen = jnp.where(
        iota(mark, 1) == iota(mark, 0) // groups, shuffle[...].astype(F32), jnp.zeros(mark, F32)
    )
    chosen = jnp.sum(chosen, axis=1, keepdims=True).astype(jnp.int32)
    square = (width, width)
    place = (iota(square, 0) % groups) * size + chosen
    selector = jnp.where(iota(square, 1) == place, 1.0, 0.0).astype(BF16)
    out[...] = dot_nt(selector, first).astype(BF16)


def second_kernel(
    shuffled,
    signal,
    weights,
    query_weight,
    key_weight,
    value_weight,
    blocks,
    resid_out,
    query_out,
    pair_out,
    source,
    spread,
    wide,
):
    groups, taps, size, _ = weights.shape
    count, width = signal.shape
    head = query_weight.shape[1]
    square = (width, width)
    row, column = iota(square, 0), iota(square, 1)
    target = ((row // groups) % groups) * size + (row // (groups * groups)) * groups + row % groups
    selector = jnp.where(column == target, 1.0, 0.0).astype(BF16)
    source[...] = dot_tn(shuffled[...], selector)
    fill_diagonal(weights, wide)
    fill_taps(source, taps, count, spread)
    second = dot(spread[...], wide[...])
    resid = (signal[...].astype(F32) + second).astype(BF16)
    resid_out[...] = resid
    queries = dot(resid, query_weight[...]).astype(BF16)
    marks = blocks[...].astype(F32)
    for member in range(query_out.shape[0]):
        query_out[member, :count, :] = queries
        query_out[member, count:, :] = jnp.concatenate(
            [
                jnp.broadcast_to(marks[:, k * head : (k + 1) * head], (EXTRA // 2, head))
                for k in range(2)
            ],
            axis=0,
        ).astype(BF16)
    pair_out[:count, :head] = dot(resid, key_weight[...]).astype(BF16)
    pair_out[:count, head:] = dot(resid, value_weight[...]).astype(BF16)
    pair_out[count:, :] = jnp.broadcast_to(marks, (EXTRA, width)).astype(BF16)


def attend_kernel(query_ref, *refs):
    pairs, out = refs[:-1], refs[-1]
    count = query_ref.shape[1] - EXTRA
    head = query_ref.shape[2]
    half = EXTRA // 2
    scale = 1.0 / math.sqrt(head)
    queries = query_ref[0, :count, :]
    marks = jnp.concatenate(
        [query_ref[0, count : count + 1, :], query_ref[0, count + half : count + half + 1, :]],
        axis=1,
    ).astype(F32)
    marks = row_to_column(marks)
    tiles = []
    peak = jnp.full((count, 1), FLOOR, F32)
    for pair in pairs:
        scores = dot_nt(queries, pair[:count, :head]) * scale
        seen = pair[count : count + 1, :].astype(F32) <= marks
        masked = jnp.where(seen, scores, NEG)
        peak = jnp.maximum(peak, jnp.max(masked, axis=1, keepdims=True))
        tiles.append(masked)
    total = jnp.zeros((count, 1), F32)
    summed = jnp.zeros((count, head), F32)
    for pair, masked in zip(pairs, tiles):
        weights = jnp.exp(masked - peak)
        total = total + jnp.sum(weights, axis=1, keepdims=True)
        summed = summed + dot(weights.astype(BF16), pair[:count, head:])
    out[0, :count, :] = summed
    peak_row, total_row = column_to_row(peak), column_to_row(total)
    out[0, count:, :] = jnp.concatenate(
        [
            peak_row[:, :head],
            peak_row[:, head:],
            total_row[:, :head],
            total_row[:, head:],
            jnp.zeros((4, head), F32),
        ],
        axis=0,
    )


def finish_kernel(parts, resid, out_weight, out):
    members = parts.shape[0]
    count = resid.shape[0]
    peaks, totals = [], []
    for member in range(members):
        rows = [parts[member, count + k : count + k + 1, :] for k in range(4)]
        peaks.append(row_to_column(jnp.concatenate(rows[:2], axis=1)))
        totals.append(row_to_column(jnp.concatenate(rows[2:], axis=1)))
    peak = functools.reduce(jnp.maximum, peaks)
    total = jnp.zeros_like(peak)
    summed = jnp.zeros((count, parts.shape[2]), F32)
    for member in range(members):
        factor = jnp.exp(peaks[member] - peak)
        total = total + factor * totals[member]
        summed = summed + factor * parts[member, :count, :]
    attended = (summed / total).astype(BF16)
    added = dot(attended, out_weight[...])
    out[...] = (resid[...].astype(F32) + added).astype(BF16)


def shape_of(shape, dtype):
    return jax.ShapeDtypeStruct(shape, dtype)


def ring_shift(rows, length, distance):
    return [
        (row * length + place, row * length + (place + distance) % length)
        for row in range(rows)
        for place in range(length)
    ]


def per_device(
    signal,
    conv_first,
    conv_second,
    shuffle,
    blocks,
    query_weight,
    key_weight,
    value_weight,
    out_weight,
):
    count, width = signal.shape
    groups, taps, size, _ = conv_first.shape
    margin = taps - 1
    padded = count + margin
    head = query_weight.shape[2]
    axis_size = lax.axis_size("tm")
    sources = lax.axis_size("freq")
    rows = 2
    length = axis_size // rows
    ring = length // 2
    members = [
        [row * length + 2 * place + parity for row in range(rows) for parity in range(2)]
        for place in range(ring)
    ]
    before = lax.ppermute(
        signal[count - 2 * margin :], "tm", [(i, i + 1) for i in range(axis_size - 1)]
    )
    permuted = pl.pallas_call(
        first_kernel,
        out_shape=shape_of((width, padded), BF16),
        scratch_shapes=[
            pltpu.VMEM((count + 2 * margin, width), F32),
            pltpu.VMEM((padded, taps * width), BF16),
            pltpu.VMEM((taps * width, width), BF16),
        ],
        name="first",
    )(signal, before, conv_first, shuffle.reshape(1, size))
    shuffled = lax.all_to_all(
        permuted.reshape(sources, width // sources, padded),
        "freq",
        split_axis=0,
        concat_axis=0,
        tiled=True,
    ).reshape(width, padded)
    resid, queries, pair = pl.pallas_call(
        second_kernel,
        out_shape=(
            shape_of((count, width), BF16),
            shape_of((2 * rows, count + EXTRA, head), BF16),
            shape_of((count + EXTRA, width), BF16),
        ),
        scratch_shapes=[
            pltpu.VMEM((padded, width), F32),
            pltpu.VMEM((count, taps * width), BF16),
            pltpu.VMEM((taps * width, width), BF16),
        ],
        name="second",
    )(
        shuffled,
        signal,
        conv_second,
        query_weight.reshape(width, head),
        key_weight.reshape(width, head),
        value_weight.reshape(width, head),
        blocks.reshape(1, count),
    )
    exchange = functools.partial(
        lax.all_to_all,
        axis_name="tm",
        split_axis=0,
        concat_axis=0,
        tiled=True,
        axis_index_groups=members,
    )
    queries = exchange(queries)
    pairs = [pair]
    ahead = behind = pair
    for step in range(ring // 2):
        ahead = lax.ppermute(ahead, "tm", ring_shift(rows, length, 2))
        pairs.append(ahead)
        if 2 * step + 2 < ring:
            behind = lax.ppermute(behind, "tm", ring_shift(rows, length, -2))
            pairs.append(behind)
    whole = pl.BlockSpec((count + EXTRA, width), lambda j: (0, 0))
    parts = pl.pallas_call(
        attend_kernel,
        grid=(2 * rows,),
        out_shape=shape_of((2 * rows, count + 8, head), F32),
        in_specs=[pl.BlockSpec((1, count + EXTRA, head), lambda j: (j, 0, 0))]
        + [whole] * len(pairs),
        out_specs=pl.BlockSpec((1, count + 8, head), lambda j: (j, 0, 0)),
        name="attend",
    )(queries, *pairs)
    parts = exchange(parts)
    return pl.pallas_call(
        finish_kernel,
        out_shape=shape_of((count, width), BF16),
        name="finish",
    )(parts, resid, out_weight.reshape(head, width))


def solution(mesh):
    in_specs = (
        P("tm", "freq"),
        P("freq", None, None, None),
        P("freq", None, None, None),
        P(),
        P("tm"),
        P("freq", None, None),
        P("freq", None, None),
        P("freq", None, None),
        P("freq", None, None),
    )
    return jax.shard_map(
        per_device, mesh=mesh, in_specs=in_specs, out_specs=P("tm", "freq"), check_vma=False
    )
```

profile of v0, /device:TPU:2, one launch (start us, length us, event | category | flops | bytes accessed | tf_op | source)
XLA Modules:
  0.0 103.8 jit_solution(11898298960640841351)
XLA Ops:
  0.0 0.7 slice.3
  0.7 3.8 %collective-permute-start = (bf16[16,256]{1,0:T(8,128)(2,1)S(1)}, bf16[16,256]{1,0:T(8,128)(2,1)S(1)}, u32[]{:S(2)}, u32[]{:S(2)}) collective-permute-start(bf16[16,256]{1,0:T(8,128)(2,1)S(1)} %slice.3), channel_id=1, source_target_pairs={{0,1},{1,2},{2,3},{3,4},{4,5},{5,6},{6,7},{7,8},{8,9},{9,10},{10,1... | collective-permute-start | bytes 24584 | tf_op jit(solution)/shard_map/ppermute | solution.py:227
  4.5 1.3 %collective-permute-done.before = bf16[16,256]{1,0:T(8,128)(2,1)S(1)} collective-permute-done((bf16[16,256]{1,0:T(8,128)(2,1)S(1)}, bf16[16,256]{1,0:T(8,128)(2,1)S(1)}, u32[]{:S(2)}, u32[]{:S(2)}) %collective-permute-start) | collective-permute-done | bytes 8224 | tf_op jit(solution)/shard_map/ppermute | solution.py:227
  5.9 0.6 copy-done.9
  6.5 2.8 %first.1 = bf16[256,264]{1,0:T(8,128)(2,1)} custom-call(bf16[256,256]{1,0:T(8,128)(2,1)} %signal.3, bf16[16,256]{1,0:T(8,128)(2,1)} %copy-done.9, bf16[4,9,64,64]{3,2,1,0:T(8,128)(2,1)} %weights.2, s32[1,64]{1,0:T(1,128)} %bitcast.15), custom_call_target="tpu_custom_call" | custom-call | tf_op jit(solution)/shard_map/first/pallas_call | solution.py:230
  9.2 14.1 %all_to_all.15 = bf16[16,16,264]{2,1,0:T(8,128)(2,1)} all-to-all(bf16[16,16,264]{2,1,0:T(8,128)(2,1)} %bitcast.9), channel_id=1, replica_groups=mesh['freq'=16,'tm'=32] {'freq'}, dimensions={0} | all-to-all | bytes 270336 | tf_op jit(solution)/shard_map/all_to_all | solution.py:240
  23.3 3.1 %second.1 = (bf16[256,256]{1,0:T(8,128)(2,1)}, bf16[4,272,128]{2,1,0:T(8,128)(2,1)}, bf16[272,256]{1,0:T(8,128)(2,1)}) custom-call(bf16[256,264]{1,0:T(8,128)(2,1)} %bitcast.8, bf16[256,256]{1,0:T(8,128)(2,1)} %signal.3, bf16[4,9,64,64]{3,2,1,0:T(8,128)(2,1)} %weights.3, bf16[256,128]{1,0:T(8,128)(2,1)} %bitcast.10, bf16[256,128]{1,0:T(8,128)(2,1)} %bitcast.11, ...), custom_call_target="tpu_custom_call" | custom-call | tf_op jit(solution)/shard_map/second/pallas_call | solution.py:247
  26.4 10.1 %all-to-all-start.1 = ((bf16[4,272,128]{2,1,0:T(8,128)(2,1)}), bf16[4,272,128]{2,1,0:T(8,128)(2,1)S(1)}, u32[]{:S(2)}, u32[]{:S(2)}) async-start(bf16[4,272,128]{2,1,0:T(8,128)(2,1)} %get-tuple-element.8), calls=%async_computation.1 | async-start | bytes 557056 | tf_op jit(solution)/shard_map/all_to_all | solution.py:277
  36.5 0.0 copy-done.1
  36.5 1.9 %collective-permute-start.1 = (bf16[272,256]{1,0:T(8,128)(2,1)S(1)}, bf16[272,256]{1,0:T(8,128)(2,1)S(1)}, u32[]{:S(2)}, u32[]{:S(2)}) collective-permute-start(bf16[272,256]{1,0:T(8,128)(2,1)S(1)} %copy-done.1), channel_id=1, source_target_pairs={{0,2},{1,3},{2,4},{3,5},{4,6},{5,7},{6,8},{7,9},{8,10},{9,11},{10,... | collective-permute-start | bytes 417800 | tf_op jit(solution)/shard_map/ppermute | solution.py:281
  38.4 6.0 %collective-permute-start.2 = (bf16[272,256]{1,0:T(8,128)(2,1)S(1)}, bf16[272,256]{1,0:T(8,128)(2,1)S(1)}, u32[]{:S(2)}, u32[]{:S(2)}) collective-permute-start(bf16[272,256]{1,0:T(8,128)(2,1)S(1)} %copy-done.1), channel_id=1, source_target_pairs={{0,14},{1,15},{2,0},{3,1},{4,2},{5,3},{6,4},{7,5},{8,6},{9,7},{10,... | collective-permute-start | bytes 417800 | tf_op jit(solution)/shard_map/ppermute | solution.py:284
  44.5 4.8 %collective-permute-done.1.refs_1_ = bf16[272,256]{1,0:T(8,128)(2,1)S(1)} collective-permute-done((bf16[272,256]{1,0:T(8,128)(2,1)S(1)}, bf16[272,256]{1,0:T(8,128)(2,1)S(1)}, u32[]{:S(2)}, u32[]{:S(2)}) %collective-permute-start.1) | collective-permute-done | bytes 139296 | tf_op jit(solution)/shard_map/ppermute | solution.py:281
  49.3 1.9 %collective-permute-start.3 = (bf16[272,256]{1,0:T(8,128)(2,1)S(1)}, bf16[272,256]{1,0:T(8,128)(2,1)S(1)}, u32[]{:S(2)}, u32[]{:S(2)}) collective-permute-start(bf16[272,256]{1,0:T(8,128)(2,1)S(1)} %collective-permute-done.1.refs_1_), channel_id=1, source_target_pairs={{0,2},{1,3},{2,4},{3,5},{4,6},{5,7},{6,8},{7,9},{8,10},{9,11},{10,... | collective-permute-start | bytes 417800 | tf_op jit(solution)/shard_map/ppermute | solution.py:281
  51.2 0.0 collective-permute-done.2.refs_2_
  51.2 0.0 copy-start.3
  51.2 6.2 %collective-permute-start.4 = (bf16[272,256]{1,0:T(8,128)(2,1)S(1)}, bf16[272,256]{1,0:T(8,128)(2,1)S(1)}, u32[]{:S(2)}, u32[]{:S(2)}) collective-permute-start(bf16[272,256]{1,0:T(8,128)(2,1)S(1)} %collective-permute-done.2.refs_2_), channel_id=1, source_target_pairs={{0,14},{1,15},{2,0},{3,1},{4,2},{5,3},{6,4},{7,5},{8,6},{9,7},{10,... | collective-permute-start | bytes 417800 | tf_op jit(solution)/shard_map/ppermute | solution.py:284
  57.4 2.0 %collective-permute-done.3.refs_3_ = bf16[272,256]{1,0:T(8,128)(2,1)S(1)} collective-permute-done((bf16[272,256]{1,0:T(8,128)(2,1)S(1)}, bf16[272,256]{1,0:T(8,128)(2,1)S(1)}, u32[]{:S(2)}, u32[]{:S(2)}) %collective-permute-start.3) | collective-permute-done | bytes 139296 | tf_op jit(solution)/shard_map/ppermute | solution.py:281
  59.4 1.9 %collective-permute-start.5 = (bf16[272,256]{1,0:T(8,128)(2,1)S(1)}, bf16[272,256]{1,0:T(8,128)(2,1)S(1)}, u32[]{:S(2)}, u32[]{:S(2)}) collective-permute-start(bf16[272,256]{1,0:T(8,128)(2,1)S(1)} %collective-permute-done.3.refs_3_), channel_id=1, source_target_pairs={{0,2},{1,3},{2,4},{3,5},{4,6},{5,7},{6,8},{7,9},{8,10},{9,11},{10,... | collective-permute-start | bytes 417800 | tf_op jit(solution)/shard_map/ppermute | solution.py:281
  61.3 1.8 %collective-permute-done.4.refs_4_ = bf16[272,256]{1,0:T(8,128)(2,1)S(1)} collective-permute-done((bf16[272,256]{1,0:T(8,128)(2,1)S(1)}, bf16[272,256]{1,0:T(8,128)(2,1)S(1)}, u32[]{:S(2)}, u32[]{:S(2)}) %collective-permute-start.4) | collective-permute-done | bytes 139296 | tf_op jit(solution)/shard_map/ppermute | solution.py:284
  63.1 6.6 %collective-permute-start.6 = (bf16[272,256]{1,0:T(8,128)(2,1)S(1)}, bf16[272,256]{1,0:T(8,128)(2,1)S(1)}, u32[]{:S(2)}, u32[]{:S(2)}) collective-permute-start(bf16[272,256]{1,0:T(8,128)(2,1)S(1)} %collective-permute-done.4.refs_4_), channel_id=1, source_target_pairs={{0,14},{1,15},{2,0},{3,1},{4,2},{5,3},{6,4},{7,5},{8,6},{9,7},{10,... | collective-permute-start | bytes 417800 | tf_op jit(solution)/shard_map/ppermute | solution.py:284
  69.7 0.0 collective-permute-done.5.refs_5_
  69.7 0.0 copy-start.6
  69.7 2.3 %collective-permute-start.7 = (bf16[272,256]{1,0:T(8,128)(2,1)S(1)}, bf16[272,256]{1,0:T(8,128)(2,1)S(1)}, u32[]{:S(2)}, u32[]{:S(2)}) collective-permute-start(bf16[272,256]{1,0:T(8,128)(2,1)S(1)} %collective-permute-done.5.refs_5_), channel_id=1, source_target_pairs={{0,2},{1,3},{2,4},{3,5},{4,6},{5,7},{6,8},{7,9},{8,10},{9,11},{10,... | collective-permute-start | bytes 417800 | tf_op jit(solution)/shard_map/ppermute | solution.py:281
  72.0 3.3 %collective-permute-done.6.refs_6_ = bf16[272,256]{1,0:T(8,128)(2,1)S(1)} collective-permute-done((bf16[272,256]{1,0:T(8,128)(2,1)S(1)}, bf16[272,256]{1,0:T(8,128)(2,1)S(1)}, u32[]{:S(2)}, u32[]{:S(2)}) %collective-permute-start.6) | collective-permute-done | bytes 139296 | tf_op jit(solution)/shard_map/ppermute | solution.py:284
  75.3 6.0 %collective-permute-done.7.refs_7_ = bf16[272,256]{1,0:T(8,128)(2,1)S(1)} collective-permute-done((bf16[272,256]{1,0:T(8,128)(2,1)S(1)}, bf16[272,256]{1,0:T(8,128)(2,1)S(1)}, u32[]{:S(2)}, u32[]{:S(2)}) %collective-permute-start.7) | collective-permute-done | bytes 139296 | tf_op jit(solution)/shard_map/ppermute | solution.py:281
  81.3 0.0 all-to-all-done.1.query_ref
  81.3 0.0 copy-done.2
  81.3 0.6 copy-done.8
  81.9 0.7 copy-done
  82.6 6.0 %attend.1 = f32[4,264,128]{2,1,0:T(8,128)} custom-call(bf16[4,272,128]{2,1,0:T(8,128)(2,1)} %copy-done, bf16[272,256]{1,0:T(8,128)(2,1)} %get-tuple-element.9.refs_0_, bf16[272,256]{1,0:T(8,128)(2,1)} %copy-done.2, bf16[272,256]{1,0:T(8,128)(2,1)} %copy-done.3, bf16[272,256]{1,0:T(8,128)(2,1)} %copy-done.4, bf16[272,256]{1,0:T(8,128)(2,1)} %copy-done.5, ...), custom_call_target="tpu_custom_call" | custom-call | tf_op jit(solution)/shard_map/attend/pallas_call | solution.py:287
  88.6 12.9 %all_to_all.16.parts = f32[4,264,128]{2,1,0:T(8,128)} all-to-all(f32[4,264,128]{2,1,0:T(8,128)} %attend.1), channel_id=1, replica_groups={{0,1,16,17},{2,3,18,19},{4,5,20,21},{6,7,22,23},{8,9,24,25},{10,11,26,2..., dimensions={0} | all-to-all | bytes 1081344 | tf_op jit(solution)/shard_map/all_to_all | solution.py:296
  101.5 2.3 %finish.1 = bf16[256,256]{1,0:T(8,128)(2,1)} custom-call(f32[4,264,128]{2,1,0:T(8,128)} %all_to_all.16.parts, bf16[256,256]{1,0:T(8,128)(2,1)} %get-tuple-element.10.resid, bf16[128,256]{1,0:T(8,128)(2,1)} %bitcast.13), custom_call_target="tpu_custom_call" | custom-call | tf_op jit(solution)/shard_map/finish/pallas_call | solution.py:297
  (13 shorter events, 0.0 us)
Async XLA Ops:
  0.7 5.2 %collective-permute-start = (bf16[16,256]{1,0:T(8,128)(2,1)S(1)}, bf16[16,256]{1,0:T(8,128)(2,1)S(1)}, u32[]{:S(2)}, u32[]{:S(2)}) collective-permute-start(bf16[16,256]{1,0:T(8,128)(2,1)S(1)} %slice.3), channel_id=1, source_target_pairs={{0,1},{1,2},{2,3},{3,4},{4,5},{5,6},{6,7},{7,8},{8,9},{9,10},{10,1... | collective-permute-start | bytes 24584 | tf_op jit(solution)/shard_map/ppermute | solution.py:227
  5.9 0.6 copy-start.9
  26.4 10.1 %copy-start.1 = (bf16[272,256]{1,0:T(8,128)(2,1)S(1)}, bf16[272,256]{1,0:T(8,128)(2,1)}, u32[]{:S(2)}) copy-start(bf16[272,256]{1,0:T(8,128)(2,1)} %get-tuple-element.9.refs_0_) | copy-start | bytes 417796
  26.4 54.9 %all-to-all-start.1 = ((bf16[4,272,128]{2,1,0:T(8,128)(2,1)}), bf16[4,272,128]{2,1,0:T(8,128)(2,1)S(1)}, u32[]{:S(2)}, u32[]{:S(2)}) async-start(bf16[4,272,128]{2,1,0:T(8,128)(2,1)} %get-tuple-element.8), calls=%async_computation.1 | async-start | bytes 557056 | tf_op jit(solution)/shard_map/all_to_all | solution.py:277
  36.5 12.8 %collective-permute-start.1 = (bf16[272,256]{1,0:T(8,128)(2,1)S(1)}, bf16[272,256]{1,0:T(8,128)(2,1)S(1)}, u32[]{:S(2)}, u32[]{:S(2)}) collective-permute-start(bf16[272,256]{1,0:T(8,128)(2,1)S(1)} %copy-done.1), channel_id=1, source_target_pairs={{0,2},{1,3},{2,4},{3,5},{4,6},{5,7},{6,8},{7,9},{8,10},{9,11},{10,... | collective-permute-start | bytes 417800 | tf_op jit(solution)/shard_map/ppermute | solution.py:281
  38.4 12.8 %collective-permute-start.2 = (bf16[272,256]{1,0:T(8,128)(2,1)S(1)}, bf16[272,256]{1,0:T(8,128)(2,1)S(1)}, u32[]{:S(2)}, u32[]{:S(2)}) collective-permute-start(bf16[272,256]{1,0:T(8,128)(2,1)S(1)} %copy-done.1), channel_id=1, source_target_pairs={{0,14},{1,15},{2,0},{3,1},{4,2},{5,3},{6,4},{7,5},{8,6},{9,7},{10,... | collective-permute-start | bytes 417800 | tf_op jit(solution)/shard_map/ppermute | solution.py:284
  49.3 32.0 %copy-start.2 = (bf16[272,256]{1,0:T(8,128)(2,1)}, bf16[272,256]{1,0:T(8,128)(2,1)S(1)}, u32[]{:S(2)}) copy-start(bf16[272,256]{1,0:T(8,128)(2,1)S(1)} %collective-permute-done.1.refs_1_) | copy-start | bytes 417796
  49.3 10.1 %collective-permute-start.3 = (bf16[272,256]{1,0:T(8,128)(2,1)S(1)}, bf16[272,256]{1,0:T(8,128)(2,1)S(1)}, u32[]{:S(2)}, u32[]{:S(2)}) collective-permute-start(bf16[272,256]{1,0:T(8,128)(2,1)S(1)} %collective-permute-done.1.refs_1_), channel_id=1, source_target_pairs={{0,2},{1,3},{2,4},{3,5},{4,6},{5,7},{6,8},{7,9},{8,10},{9,11},{10,... | collective-permute-start | bytes 417800 | tf_op jit(solution)/shard_map/ppermute | solution.py:281
  51.2 30.0 %copy-start.3 = (bf16[272,256]{1,0:T(8,128)(2,1)}, bf16[272,256]{1,0:T(8,128)(2,1)S(1)}, u32[]{:S(2)}) copy-start(bf16[272,256]{1,0:T(8,128)(2,1)S(1)} %collective-permute-done.2.refs_2_) | copy-start | bytes 417796
  51.2 11.8 %collective-permute-start.4 = (bf16[272,256]{1,0:T(8,128)(2,1)S(1)}, bf16[272,256]{1,0:T(8,128)(2,1)S(1)}, u32[]{:S(2)}, u32[]{:S(2)}) collective-permute-start(bf16[272,256]{1,0:T(8,128)(2,1)S(1)} %collective-permute-done.2.refs_2_), channel_id=1, source_target_pairs={{0,14},{1,15},{2,0},{3,1},{4,2},{5,3},{6,4},{7,5},{8,6},{9,7},{10,... | collective-permute-start | bytes 417800 | tf_op jit(solution)/shard_map/ppermute | solution.py:284
  59.4 21.9 %copy-start.4 = (bf16[272,256]{1,0:T(8,128)(2,1)}, bf16[272,256]{1,0:T(8,128)(2,1)S(1)}, u32[]{:S(2)}) copy-start(bf16[272,256]{1,0:T(8,128)(2,1)S(1)} %collective-permute-done.3.refs_3_) | copy-start | bytes 417796
  59.4 10.3 %collective-permute-start.5 = (bf16[272,256]{1,0:T(8,128)(2,1)S(1)}, bf16[272,256]{1,0:T(8,128)(2,1)S(1)}, u32[]{:S(2)}, u32[]{:S(2)}) collective-permute-start(bf16[272,256]{1,0:T(8,128)(2,1)S(1)} %collective-permute-done.3.refs_3_), channel_id=1, source_target_pairs={{0,2},{1,3},{2,4},{3,5},{4,6},{5,7},{6,8},{7,9},{8,10},{9,11},{10,... | collective-permute-start | bytes 417800 | tf_op jit(solution)/shard_map/ppermute | solution.py:281
  63.1 18.2 %copy-start.5 = (bf16[272,256]{1,0:T(8,128)(2,1)}, bf16[272,256]{1,0:T(8,128)(2,1)S(1)}, u32[]{:S(2)}) copy-start(bf16[272,256]{1,0:T(8,128)(2,1)S(1)} %collective-permute-done.4.refs_4_) | copy-start | bytes 417796
  63.1 12.2 %collective-permute-start.6 = (bf16[272,256]{1,0:T(8,128)(2,1)S(1)}, bf16[272,256]{1,0:T(8,128)(2,1)S(1)}, u32[]{:S(2)}, u32[]{:S(2)}) collective-permute-start(bf16[272,256]{1,0:T(8,128)(2,1)S(1)} %collective-permute-done.4.refs_4_), channel_id=1, source_target_pairs={{0,14},{1,15},{2,0},{3,1},{4,2},{5,3},{6,4},{7,5},{8,6},{9,7},{10,... | collective-permute-start | bytes 417800 | tf_op jit(solution)/shard_map/ppermute | solution.py:284
  69.7 11.6 %copy-start.6 = (bf16[272,256]{1,0:T(8,128)(2,1)}, bf16[272,256]{1,0:T(8,128)(2,1)S(1)}, u32[]{:S(2)}) copy-start(bf16[272,256]{1,0:T(8,128)(2,1)S(1)} %collective-permute-done.5.refs_5_) | copy-start | bytes 417796
  69.7 11.6 %collective-permute-start.7 = (bf16[272,256]{1,0:T(8,128)(2,1)S(1)}, bf16[272,256]{1,0:T(8,128)(2,1)S(1)}, u32[]{:S(2)}, u32[]{:S(2)}) collective-permute-start(bf16[272,256]{1,0:T(8,128)(2,1)S(1)} %collective-permute-done.5.refs_5_), channel_id=1, source_target_pairs={{0,2},{1,3},{2,4},{3,5},{4,6},{5,7},{6,8},{7,9},{8,10},{9,11},{10,... | collective-permute-start | bytes 417800 | tf_op jit(solution)/shard_map/ppermute | solution.py:281
  75.2 6.1 %copy-start.7 = (bf16[272,256]{1,0:T(8,128)(2,1)}, bf16[272,256]{1,0:T(8,128)(2,1)S(1)}, u32[]{:S(2)}) copy-start(bf16[272,256]{1,0:T(8,128)(2,1)S(1)} %collective-permute-done.6.refs_6_) | copy-start | bytes 417796
  81.3 0.7 copy-start.8
  81.9 0.7 copy-start
where the time goes:
time: 105 us; the launch traced here: 104 us
  starting transfers between devices  40.7 us (39%)
  blocking collectives  27 us (26%)
  waiting for transfers between devices  19.3 us (18%)
  Pallas kernels  14.1 us (13%)
  local copies, waits for them, and re-layouts  2.62 us (2%)
    ppermute x3, starting transfers between devices, per_device(): behind = lax.ppermute(behind, 'tm', ring_shift(rows, length, -2))  18.7 us
    all_to_all x1, blocking collectives, per_device(): lax.all_to_all(permuted.reshape(sources, width // sources, padded), 'freq...  14.1 us
    all_to_all x1, blocking collectives, per_device(): parts = exchange(parts)  12.9 us
    ppermute x4, waiting for transfers between devices, per_device(): ahead = lax.ppermute(ahead, 'tm', ring_shift(rows, length, 2))  12.9 us
    all_to_all x1, starting transfers between devices, per_device(): queries = exchange(queries)  10.1 us
    ppermute x4, starting transfers between devices, per_device(): ahead = lax.ppermute(ahead, 'tm', ring_shift(rows, length, 2))  8 us
    pallas_call x1, Pallas kernels, per_device(): pl.pallas_call(attend_kernel, grid=(2 * rows,), out_shape=shape_of((2 * r...  5.98 us
    ppermute x3, waiting for transfers between devices, per_device(): behind = lax.ppermute(behind, 'tm', ring_shift(rows, length, -2))  5.05 us
  transfers between devices with their start and end apart: 9, of which 6 were waited for; matrix products, arithmetic and copies ran while one was open for 0% of the time, Pallas kernels for 0%

commit v1 on v0

v1 whole, which is shorter than its diff:
```python
import functools
import math

import jax
import jax.numpy as jnp
from jax import lax
from jax.experimental import pallas as pl
from jax.experimental.pallas import tpu as pltpu
from jax.sharding import PartitionSpec as P


F32 = jnp.float32
BF16 = jnp.bfloat16
NEG = -1e30
FLOOR = -1e28
TINY = 1e-30
EXTRA = 8
STATS = 16
LIMIT = 24 * 1024 * 1024


def dot(a, b):
    return lax.dot_general(a, b, (((1,), (0,)), ((), ())), preferred_element_type=F32)


def dot_nt(a, b):
    return lax.dot_general(a, b, (((1,), (1,)), ((), ())), preferred_element_type=F32)


def dot_tn(a, b):
    return lax.dot_general(a, b, (((0,), (0,)), ((), ())), preferred_element_type=F32)


def iota(shape, dim):
    return lax.broadcasted_iota(jnp.int32, shape, dim)


def row_to_column(row):
    size = row.shape[1]
    square = (size, size)
    kept = jnp.where(iota(square, 0) == iota(square, 1), row, jnp.zeros_like(row))
    return jnp.sum(kept, axis=1, keepdims=True)


def column_to_row(column):
    size = column.shape[0]
    square = (size, size)
    kept = jnp.where(iota(square, 0) == iota(square, 1), column, jnp.zeros_like(column))
    return jnp.sum(kept, axis=0, keepdims=True)


def fill_diagonal(weights, wide):
    groups, taps, rows, columns = weights.shape
    width = groups * rows
    wide[...] = jnp.zeros_like(wide)
    for tap in range(taps):
        for group in range(groups):
            top = tap * width + group * rows
            wide[top : top + rows, group * columns : (group + 1) * columns] = weights[group, tap]


def fill_taps(source, taps, count, spread):
    width = source.shape[1]
    for tap in range(taps):
        start = taps - 1 - tap
        spread[:, tap * width : (tap + 1) * width] = source[start : start + count, :].astype(BF16)


def prepare_kernel(first, second, shuffle, first_wide, second_wide, send, receive):
    groups, _, size, _ = first.shape
    width = groups * size
    fill_diagonal(first, first_wide)
    fill_diagonal(second, second_wide)
    mark = (width, size)
    chosen = jnp.where(
        iota(mark, 1) == iota(mark, 0) // groups, shuffle[...].astype(F32), jnp.zeros(mark, F32)
    )
    chosen = jnp.sum(chosen, axis=1, keepdims=True).astype(jnp.int32)
    square = (width, width)
    row, column = iota(square, 0), iota(square, 1)
    place = (row % groups) * size + chosen
    send[...] = jnp.where(column == place, 1.0, 0.0).astype(BF16)
    target = ((row // groups) % groups) * size + (row // (groups * groups)) * groups + row % groups
    receive[...] = jnp.where(column == target, 1.0, 0.0).astype(BF16)


def first_kernel(taps, signal, before, wide, send, out, source, spread):
    count = signal.shape[0]
    margin = taps - 1
    source[: 2 * margin, :] = before[...].astype(F32)
    source[2 * margin :, :] = signal[...].astype(F32)
    fill_taps(source, taps, count + margin, spread)
    total = dot(spread[...], wide[...])
    first = (total / (1.0 + jnp.exp(-total))).astype(BF16)
    out[...] = dot_nt(send[...], first).astype(BF16)


def second_kernel(
    taps,
    shuffled,
    signal,
    wide,
    receive,
    query_weight,
    key_weight,
    value_weight,
    blocks,
    resid_out,
    query_out,
    pair_out,
    source,
    spread,
):
    count, width = signal.shape
    head = query_weight.shape[1]
    source[...] = dot_tn(shuffled[...], receive[...])
    fill_taps(source, taps, count, spread)
    second = dot(spread[...], wide[...])
    resid = (signal[...].astype(F32) + second).astype(BF16)
    resid_out[...] = resid
    queries = dot(resid, query_weight[...]).astype(BF16)
    marks = blocks[...].astype(F32)
    extra = jnp.concatenate(
        [
            jnp.broadcast_to(marks[:, k * head : (k + 1) * head], (EXTRA // 2, head))
            for k in range(2)
        ],
        axis=0,
    ).astype(BF16)
    for member in range(query_out.shape[0]):
        query_out[member, :count, :] = queries
        query_out[member, count:, :] = extra
    pair_out[:count, :head] = dot(resid, key_weight[...]).astype(BF16)
    pair_out[:count, head:] = dot(resid, value_weight[...]).astype(BF16)
    pair_out[count:, :] = jnp.broadcast_to(marks, (EXTRA, width)).astype(BF16)


def split_three(value):
    pieces = []
    for _ in range(3):
        piece = value.astype(BF16).astype(F32)
        pieces.append(piece)
        value = value - piece
    return pieces


def attend_kernel(held, fresh, last, *refs):
    query_ref, pairs = refs[0], refs[1 : 1 + fresh]
    old = refs[1 + fresh : 1 + fresh + held]
    outs = refs[1 + fresh + held :]
    members, count, head = query_ref.shape
    count = count - EXTRA
    half = EXTRA // 2
    scale = math.log2(math.e) / math.sqrt(head)
    shape = (count, head)
    halves = count // head
    for member in range(members):
        queries = query_ref[member, :count, :]
        if held:
            marks, before = old[0][member], old[1][member]
        else:
            marks = jnp.concatenate(
                [
                    query_ref[member, count : count + 1, :],
                    query_ref[member, count + half : count + half + 1, :],
                ],
                axis=1,
            ).astype(F32)
            marks = jnp.broadcast_to(row_to_column(marks), shape)
            before = jnp.full(shape, FLOOR, F32)
        tiles = []
        most = before
        for pair in pairs:
            scores = dot_nt(queries, pair[:count, :head])
            for part in range(halves):
                span = slice(part * head, (part + 1) * head)
                seen = pair[count : count + 1, span].astype(F32) <= marks
                masked = jnp.where(seen, scores[:, span], NEG)
                most = jnp.maximum(most, masked)
                tiles.append(masked)
        peak = jnp.broadcast_to(jnp.max(most, axis=1, keepdims=True), shape)
        summed = added = jnp.zeros(shape, F32)
        if held:
            factor = jnp.exp2((before - peak) * scale)
            summed = old[3][member] * factor
        for index, pair in enumerate(pairs):
            weights = []
            for masked in tiles[index * halves : (index + 1) * halves]:
                weights.append(jnp.exp2((masked - peak) * scale))
                added = added + weights[-1]
            weights = jnp.concatenate([w.astype(BF16) for w in weights], axis=1)
            summed = summed + dot(weights, pair[:count, head:])
        total = jnp.broadcast_to(jnp.sum(added, axis=1, keepdims=True), shape)
        if held:
            total = total + old[2][member] * factor
        if last:
            shared = summed / jnp.maximum(total, TINY)
            outs[0][member, :count, :] = shared.astype(BF16)
            rows = []
            for column in (peak, total):
                for piece in split_three(column_to_row(column[:, :1])):
                    rows += [piece[:, :head], piece[:, head:]]
            rows.append(jnp.zeros((STATS - len(rows), head), F32))
            outs[0][member, count:, :] = jnp.concatenate(rows, axis=0).astype(BF16)

            @pl.when(own_member() == member)
            def _():
                outs[1][...] = shared

        else:
            outs[0][member] = marks
            outs[1][member] = peak
            outs[2][member] = total
            outs[3][member] = summed


def own_member():
    place = lax.axis_index("tm")
    return 2 * (place // (lax.axis_size("tm") // 2)) + place % 2


def finish_kernel(parts, own, resid, out_weight, out):
    members = parts.shape[0]
    count = resid.shape[0]
    head = parts.shape[2]
    scale = math.log2(math.e) / math.sqrt(head)
    peaks, totals = [], []
    for member in range(members):
        stats = parts[member, count:, :].astype(F32)
        for index, kept in ((0, peaks), (6, totals)):
            pieces = [
                jnp.concatenate([stats[k : k + 1], stats[k + 1 : k + 2]], axis=1)
                for k in range(index, index + 6, 2)
            ]
            kept.append(pieces[0] + (pieces[1] + pieces[2]))
    peak = functools.reduce(jnp.maximum, peaks)
    shares = [jnp.exp2((peaks[k] - peak) * scale) * totals[k] for k in range(members)]
    whole = functools.reduce(jnp.add, shares)
    summed = jnp.zeros((count, head), F32)
    for member in range(members):
        share = row_to_column(shares[member] / whole)
        part = jnp.where(
            own_member() == member, own[...], parts[member, :count, :].astype(F32)
        )
        summed = summed + share * part
    added = dot(summed.astype(BF16), out_weight[...])
    out[...] = (resid[...].astype(F32) + added).astype(BF16)


def near(array):
    return pltpu.with_memory_space_constraint(array, pltpu.VMEM)


def call(kernel, outs, inputs, scratch=(), place=near):
    spec = pl.BlockSpec(memory_space=pltpu.VMEM) if place is near else pl.BlockSpec()
    return pl.pallas_call(
        kernel,
        out_shape=outs,
        in_specs=[spec] * len(inputs),
        out_specs=jax.tree.map(lambda _: pl.BlockSpec(memory_space=pltpu.VMEM), outs),
        scratch_shapes=scratch,
        compiler_params=pltpu.CompilerParams(vmem_limit_bytes=LIMIT if place is near else None),
    )(*[place(array) for array in inputs])


def ring_shift(rows, length, distance):
    return [
        (row * length + place, row * length + (place + distance) % length)
        for row in range(rows)
        for place in range(length)
    ]


def per_device(
    signal,
    conv_first,
    conv_second,
    shuffle,
    blocks,
    query_weight,
    key_weight,
    value_weight,
    out_weight,
):
    count, width = signal.shape
    _, taps, size, _ = conv_first.shape
    margin = taps - 1
    padded = count + margin
    head = query_weight.shape[2]
    axis_size = lax.axis_size("tm")
    sources = lax.axis_size("freq")
    rows = 2
    length = axis_size // rows
    ring = length // 2
    members = [
        [row * length + 2 * place + parity for row in range(rows) for parity in range(2)]
        for place in range(ring)
    ]
    before = lax.ppermute(
        signal[count - 2 * margin :], "tm", [(i, i + 1) for i in range(axis_size - 1)]
    )
    first_wide, second_wide, send, receive = call(
        prepare_kernel,
        [
            pltpu.VMEM((taps * width, width), BF16),
            pltpu.VMEM((taps * width, width), BF16),
            pltpu.VMEM((width, width), BF16),
            pltpu.VMEM((width, width), BF16),
        ],
        (conv_first, conv_second, shuffle.reshape(1, size)),
        place=lambda array: array,
    )
    (permuted,) = call(
        functools.partial(first_kernel, taps),
        [pltpu.VMEM((width, padded), BF16)],
        (signal, before, first_wide, send),
        [
            pltpu.VMEM((count + 2 * margin, width), F32),
            pltpu.VMEM((padded, taps * width), BF16),
        ],
    )
    shuffled = lax.all_to_all(
        permuted.reshape(sources, width // sources, padded),
        "freq",
        split_axis=0,
        concat_axis=0,
        tiled=True,
    ).reshape(width, padded)
    resid, queries, pair = call(
        functools.partial(second_kernel, taps),
        [
            pltpu.VMEM((count, width), BF16),
            pltpu.VMEM((2 * rows, count + EXTRA, head), BF16),
            pltpu.VMEM((count + EXTRA, width), BF16),
        ],
        (
            shuffled,
            signal,
            second_wide,
            receive,
            query_weight.reshape(width, head),
            key_weight.reshape(width, head),
            value_weight.reshape(width, head),
            blocks.reshape(1, count),
        ),
        [
            pltpu.VMEM((padded, width), F32),
            pltpu.VMEM((count, taps * width), BF16),
        ],
    )
    exchange = functools.partial(
        lax.all_to_all,
        axis_name="tm",
        split_axis=0,
        concat_axis=0,
        tiled=True,
        axis_index_groups=members,
    )
    state_shapes = [pltpu.VMEM((2 * rows, count, head), F32)] * 4
    last_shapes = [
        pltpu.VMEM((2 * rows, count + STATS, head), BF16),
        pltpu.VMEM((count, head), F32),
    ]

    def attend(state, fresh, last=False):
        return call(
            functools.partial(attend_kernel, len(state), len(fresh), last),
            last_shapes if last else state_shapes,
            (queries, *fresh, *state),
        )

    state, fresh = (), [pair]
    ahead = behind = pair
    for step in range(ring // 2):
        ahead = lax.ppermute(ahead, "tm", ring_shift(rows, length, 2))
        both = 2 * step + 2 < ring
        if both:
            behind = lax.ppermute(behind, "tm", ring_shift(rows, length, -2))
        if step == 0:
            queries = exchange(queries)
        else:
            state = attend(state, fresh)
            fresh = []
            if step + 1 < ring // 2:
                behind, *state = lax.optimization_barrier((behind, *state))
        fresh = fresh + ([ahead, behind] if both else [ahead])
    state = attend(state, fresh, last=True)
    parts = exchange(state[0])
    return pl.pallas_call(
        finish_kernel,
        out_shape=jax.ShapeDtypeStruct((count, width), BF16),
        name="finish",
    )(near(parts), near(state[1]), near(resid), near(out_weight.reshape(head, width)))


def solution(mesh):
    in_specs = (
        P("tm", "freq"),
        P("freq", None, None, None),
        P("freq", None, None, None),
        P(),
        P("tm"),
        P("freq", None, None),
        P("freq", None, None),
        P("freq", None, None),
        P("freq", None, None),
    )

    return jax.shard_map(
        per_device, mesh=mesh, in_specs=in_specs, out_specs=P("tm", "freq"), check_vma=False
    )
```

time: 105 us -> 90.4 us (0.86)
  the two profiles are of different devices: /device:TPU:2 before, /device:TPU:1 now
where the time goes in v1:
time: 90.4 us; the launch traced here: 89.9 us
  starting transfers between devices  37.7 us (42%)
  blocking collectives  31.8 us (35%)
  Pallas kernels  12.1 us (13%)
  waiting for transfers between devices  7.29 us (8%)
    ppermute x3, starting transfers between devices, per_device(): behind = lax.ppermute(behind, 'tm', ring_shift(rows, length, -2))  16.6 us
    all_to_all x1, blocking collectives, per_device(): parts = exchange(state[0])  16 us
    all_to_all x1, blocking collectives, per_device(): lax.all_to_all(permuted.reshape(sources, width // sources, padded), 'freq...  15.8 us
    pallas_call x7, Pallas kernels, call(): pl.pallas_call(kernel, out_shape=outs, in_specs=[spec] * len(inputs), out...  11.1 us
    all_to_all x1, starting transfers between devices, per_device(): queries = exchange(queries)  9.05 us
    ppermute x4, starting transfers between devices, per_device(): ahead = lax.ppermute(ahead, 'tm', ring_shift(rows, length, 2))  7.65 us
    ppermute x4, waiting for transfers between devices, per_device(): ahead = lax.ppermute(ahead, 'tm', ring_shift(rows, length, 2))  7.27 us
    ppermute x1, starting transfers between devices, per_device(): lax.ppermute(signal[count - 2 * margin:], 'tm', [(i, i + 1) for i in rang...  4.35 us
  transfers between devices with their start and end apart: 9, of which 3 were waited for; matrix products, arithmetic and copies ran while one was open for 0% of the time, Pallas kernels for 8%

profile of v1, /device:TPU:1, one launch (start us, length us, event | category | flops | bytes accessed | tf_op | source)
XLA Modules:
  0.0 89.9 jit_solution(1626440357288216027)
XLA Ops:
  0.0 0.8 slice.3
  0.8 4.3 %collective-permute-start = (bf16[16,256]{1,0:T(8,128)(2,1)S(1)}, bf16[16,256]{1,0:T(8,128)(2,1)S(1)}, u32[]{:S(2)}, u32[]{:S(2)}) collective-permute-start(bf16[16,256]{1,0:T(8,128)(2,1)S(1)} %slice.3), channel_id=1, source_target_pairs={{0,1},{1,2},{2,3},{3,4},{4,5},{5,6},{6,7},{7,8},{8,9},{9,10},{10,1... | collective-permute-start | bytes 24584 | tf_op jit(solution)/shard_map/ppermute | solution.py:299
  5.1 1.9 %shard_map.91 = (bf16[2304,256]{1,0:T(8,128)(2,1)S(1)}, bf16[2304,256]{1,0:T(8,128)(2,1)S(1)}, bf16[256,256]{1,0:T(8,128)(2,1)S(1)}, bf16[256,256]{1,0:T(8,128)(2,1)S(1)}) custom-call(bf16[4,9,64,64]{3,2,1,0:T(8,128)(2,1)} %first.1, bf16[4,9,64,64]{3,2,1,0:T(8,128)(2,1)} %second.1, s32[1,64]{1,0:T(1,128)} %bitcast.15), custom_call_target="tpu_custom_call" | custom-call | tf_op jit(solution)/shard_map/pallas_call | solution.py:256
  7.1 0.0 copy-start.1
  7.1 0.0 copy-start.2
  7.1 0.0 copy-start.3
  7.1 0.0 copy-start.5
  7.1 0.0 collective-permute-done.before
  7.1 0.8 shard_map.92
  8.0 15.8 %all_to_all.15 = bf16[16,16,264]{2,1,0:T(8,128)(2,1)S(1)} all-to-all(bf16[16,16,264]{2,1,0:T(8,128)(2,1)S(1)} %bitcast.9), channel_id=1, replica_groups=mesh['freq'=16,'tm'=32] {'freq'}, dimensions={0} | all-to-all | bytes 270336 | tf_op jit(solution)/shard_map/all_to_all | solution.py:322
  23.8 1.6 %shard_map.93 = (bf16[256,256]{1,0:T(8,128)(2,1)S(1)}, bf16[4,264,128]{2,1,0:T(8,128)(2,1)}, bf16[264,256]{1,0:T(8,128)(2,1)S(1)}) custom-call(bf16[256,264]{1,0:T(8,128)(2,1)S(1)} %bitcast.8, bf16[256,256]{1,0:T(8,128)(2,1)S(1)} %copy-done, bf16[2304,256]{1,0:T(8,128)(2,1)S(1)} %get-tuple-element.38.wide, bf16[256,256]{1,0:T(8,128)(2,1)S(1)} %get-tuple-element.39.receive, ...), custom_call_target="tpu_custom_call" | custom-call | tf_op jit(solution)/shard_map/pallas_call | solution.py:256
  25.4 9.0 %all-to-all-start.1 = ((bf16[4,264,128]{2,1,0:T(8,128)(2,1)}), bf16[4,264,128]{2,1,0:T(8,128)(2,1)S(1)}, u32[]{:S(2)}, u32[]{:S(2)}) async-start(bf16[4,264,128]{2,1,0:T(8,128)(2,1)} %get-tuple-element.40), calls=%async_computation.1 | async-start | bytes 540672 | tf_op jit(solution)/shard_map/all_to_all | solution.py:380
  34.5 1.9 %collective-permute-start.1 = (bf16[264,256]{1,0:T(8,128)(2,1)S(1)}, bf16[264,256]{1,0:T(8,128)(2,1)S(1)}, u32[]{:S(2)}, u32[]{:S(2)}) collective-permute-start(bf16[264,256]{1,0:T(8,128)(2,1)S(1)} %get-tuple-element.41.refs_1_), channel_id=1, source_target_pairs={{0,2},{1,3},{2,4},{3,5},{4,6},{5,7},{6,8},{7,9},{8,10},{9,11},{10,... | collective-permute-start | bytes 405512 | tf_op jit(solution)/shard_map/ppermute | solution.py:375
  36.4 5.7 %collective-permute-start.5 = (bf16[264,256]{1,0:T(8,128)(2,1)S(1)}, bf16[264,256]{1,0:T(8,128)(2,1)S(1)}, u32[]{:S(2)}, u32[]{:S(2)}) collective-permute-start(bf16[264,256]{1,0:T(8,128)(2,1)S(1)} %get-tuple-element.41.refs_1_), channel_id=1, source_target_pairs={{0,14},{1,15},{2,0},{3,1},{4,2},{5,3},{6,4},{7,5},{8,6},{9,7},{10,... | collective-permute-start | bytes 405512 | tf_op jit(solution)/shard_map/ppermute | solution.py:378
  42.1 3.7 %collective-permute-done.1.refs_2_ = bf16[264,256]{1,0:T(8,128)(2,1)S(1)} collective-permute-done((bf16[264,256]{1,0:T(8,128)(2,1)S(1)}, bf16[264,256]{1,0:T(8,128)(2,1)S(1)}, u32[]{:S(2)}, u32[]{:S(2)}) %collective-permute-start.1) | collective-permute-done | bytes 135200 | tf_op jit(solution)/shard_map/ppermute | solution.py:375
  45.8 1.9 %collective-permute-start.2 = (bf16[264,256]{1,0:T(8,128)(2,1)S(1)}, bf16[264,256]{1,0:T(8,128)(2,1)S(1)}, u32[]{:S(2)}, u32[]{:S(2)}) collective-permute-start(bf16[264,256]{1,0:T(8,128)(2,1)S(1)} %collective-permute-done.1.refs_2_), channel_id=1, source_target_pairs={{0,2},{1,3},{2,4},{3,5},{4,6},{5,7},{6,8},{7,9},{8,10},{9,11},{10,... | collective-permute-start | bytes 405512 | tf_op jit(solution)/shard_map/ppermute | solution.py:375
  47.7 0.0 collective-permute-done.5.refs_3_
  47.7 5.5 %collective-permute-start.6 = (bf16[264,256]{1,0:T(8,128)(2,1)S(1)}, bf16[264,256]{1,0:T(8,128)(2,1)S(1)}, u32[]{:S(2)}, u32[]{:S(2)}) collective-permute-start(bf16[264,256]{1,0:T(8,128)(2,1)S(1)} %collective-permute-done.5.refs_3_), channel_id=1, source_target_pairs={{0,14},{1,15},{2,0},{3,1},{4,2},{5,3},{6,4},{7,5},{8,6},{9,7},{10,... | collective-permute-start | bytes 405512 | tf_op jit(solution)/shard_map/ppermute | solution.py:378
  53.2 0.5 collective-permute-done.2.refs_1_
  53.7 1.9 %collective-permute-start.3 = (bf16[264,256]{1,0:T(8,128)(2,1)S(1)}, bf16[264,256]{1,0:T(8,128)(2,1)S(1)}, u32[]{:S(2)}, u32[]{:S(2)}) collective-permute-start(bf16[264,256]{1,0:T(8,128)(2,1)S(1)} %collective-permute-done.2.refs_1_), channel_id=1, source_target_pairs={{0,2},{1,3},{2,4},{3,5},{4,6},{5,7},{6,8},{7,9},{8,10},{9,11},{10,... | collective-permute-start | bytes 405512 | tf_op jit(solution)/shard_map/ppermute | solution.py:375
  55.6 2.0 %shard_map.94 = (f32[4,256,128]{2,1,0:T(8,128)S(1)}, f32[4,256,128]{2,1,0:T(8,128)S(1)}, f32[4,256,128]{2,1,0:T(8,128)S(1)}, f32[4,256,128]{2,1,0:T(8,128)S(1)}) custom-call(bf16[4,264,128]{2,1,0:T(8,128)(2,1)S(1)} %all-to-all-done.1.refs_0_, bf16[264,256]{1,0:T(8,128)(2,1)S(1)} %get-tuple-element.41.refs_1_, ...), custom_call_target="tpu_custom_call" | custom-call | tf_op jit(solution)/shard_map/pallas_call | solution.py:256
  57.6 0.0 collective-permute-done.6.refs_2_
  57.6 5.5 %collective-permute-start.7 = (bf16[264,256]{1,0:T(8,128)(2,1)S(1)}, bf16[264,256]{1,0:T(8,128)(2,1)S(1)}, u32[]{:S(2)}, u32[]{:S(2)}) collective-permute-start(bf16[264,256]{1,0:T(8,128)(2,1)S(1)} %collective-permute-done.6.refs_2_), channel_id=1, source_target_pairs={{0,14},{1,15},{2,0},{3,1},{4,2},{5,3},{6,4},{7,5},{8,6},{9,7},{10,... | collective-permute-start | bytes 405512 | tf_op jit(solution)/shard_map/ppermute | solution.py:378
  63.1 0.0 collective-permute-done.3.refs_1_
  63.1 1.9 %collective-permute-start.4 = (bf16[264,256]{1,0:T(8,128)(2,1)S(1)}, bf16[264,256]{1,0:T(8,128)(2,1)S(1)}, u32[]{:S(2)}, u32[]{:S(2)}) collective-permute-start(bf16[264,256]{1,0:T(8,128)(2,1)S(1)} %collective-permute-done.3.refs_1_), channel_id=1, source_target_pairs={{0,2},{1,3},{2,4},{3,5},{4,6},{5,7},{6,8},{7,9},{8,10},{9,11},{10,... | collective-permute-start | bytes 405512 | tf_op jit(solution)/shard_map/ppermute | solution.py:375
  65.0 1.4 %shard_map.95 = (f32[4,256,128]{2,1,0:T(8,128)S(1)}, f32[4,256,128]{2,1,0:T(8,128)S(1)}, f32[4,256,128]{2,1,0:T(8,128)S(1)}, f32[4,256,128]{2,1,0:T(8,128)S(1)}) custom-call(bf16[4,264,128]{2,1,0:T(8,128)(2,1)S(1)} %all-to-all-done.1.refs_0_, bf16[264,256]{1,0:T(8,128)(2,1)S(1)} %collective-permute-done.2.refs_1_, ...), custom_call_target="tpu_custom_call" | custom-call | tf_op jit(solution)/shard_map/pallas_call | solution.py:256
  66.5 0.0 collective-permute-done.7.refs_2_
  66.5 1.4 %shard_map.96 = (f32[4,256,128]{2,1,0:T(8,128)S(1)}, f32[4,256,128]{2,1,0:T(8,128)S(1)}, f32[4,256,128]{2,1,0:T(8,128)S(1)}, f32[4,256,128]{2,1,0:T(8,128)S(1)}) custom-call(bf16[4,264,128]{2,1,0:T(8,128)(2,1)S(1)} %all-to-all-done.1.refs_0_, bf16[264,256]{1,0:T(8,128)(2,1)S(1)} %collective-permute-done.3.refs_1_, ...), custom_call_target="tpu_custom_call" | custom-call | tf_op jit(solution)/shard_map/pallas_call | solution.py:256
  67.9 3.0 %collective-permute-done.4.refs_1_ = bf16[264,256]{1,0:T(8,128)(2,1)S(1)} collective-permute-done((bf16[264,256]{1,0:T(8,128)(2,1)S(1)}, bf16[264,256]{1,0:T(8,128)(2,1)S(1)}, u32[]{:S(2)}, u32[]{:S(2)}) %collective-permute-start.4) | collective-permute-done | bytes 135200 | tf_op jit(solution)/shard_map/ppermute | solution.py:375
  71.0 1.9 %shard_map.97 = (bf16[4,272,128]{2,1,0:T(8,128)(2,1)S(1)}, f32[256,128]{1,0:T(8,128)S(1)}) custom-call(bf16[4,264,128]{2,1,0:T(8,128)(2,1)S(1)} %all-to-all-done.1.refs_0_, bf16[264,256]{1,0:T(8,128)(2,1)S(1)} %collective-permute-done.4.refs_1_, f32[4,256,128]{2,1,0:T(8,128)S(1)} %get-tuple-element.60.refs_2_, f32[4,256,128]{2,1,0:T(8,128)S(1)} %get-tuple-element.61.refs_3_, ...), custom_call_target="tpu_custom_call" | custom-call | tf_op jit(solution)/shard_map/pallas_call | solution.py:256
  72.9 16.0 %all_to_all.16.parts = bf16[4,272,128]{2,1,0:T(8,128)(2,1)S(1)} all-to-all(bf16[4,272,128]{2,1,0:T(8,128)(2,1)S(1)} %get-tuple-element.64), channel_id=1, replica_groups={{0,1,16,17},{2,3,18,19},{4,5,20,21},{6,7,22,23},{8,9,24,25},{10,11,26,2..., dimensions={0} | all-to-all | bytes 557056 | tf_op jit(solution)/shard_map/all_to_all | solution.py:388
  88.9 1.0 %finish.1 = bf16[256,256]{1,0:T(8,128)(2,1)} custom-call(bf16[4,272,128]{2,1,0:T(8,128)(2,1)S(1)} %all_to_all.16.parts, f32[256,128]{1,0:T(8,128)S(1)} %get-tuple-element.65.own, bf16[256,256]{1,0:T(8,128)(2,1)S(1)} %get-tuple-element.66.resid, bf16[128,256]{1,0:T(8,128)(2,1)S(1)} %bitcast.13), custom_call_target="tpu_custom_call" | custom-call | tf_op jit(solution)/shard_map/finish/pallas_call | solution.py:389
  (9 shorter events, 0.0 us)
Async XLA Ops:
  0.0 7.1 %copy-start = (bf16[256,256]{1,0:T(8,128)(2,1)S(1)}, bf16[256,256]{1,0:T(8,128)(2,1)}, u32[]{:S(2)}) copy-start(bf16[256,256]{1,0:T(8,128)(2,1)} %signal.3) | copy-start | bytes 393220
  0.8 6.3 %collective-permute-start = (bf16[16,256]{1,0:T(8,128)(2,1)S(1)}, bf16[16,256]{1,0:T(8,128)(2,1)S(1)}, u32[]{:S(2)}, u32[]{:S(2)}) collective-permute-start(bf16[16,256]{1,0:T(8,128)(2,1)S(1)} %slice.3), channel_id=1, source_target_pairs={{0,1},{1,2},{2,3},{3,4},{4,5},{5,6},{6,7},{7,8},{8,9},{9,10},{10,1... | collective-permute-start | bytes 24584 | tf_op jit(solution)/shard_map/ppermute | solution.py:299
  7.1 16.7 %copy-start.1 = (bf16[1,256,128]{2,1,0:T(8,128)(2,1)S(1)}, bf16[1,256,128]{2,1,0:T(8,128)(2,1)}, u32[]{:S(2)}) copy-start(bf16[1,256,128]{2,1,0:T(8,128)(2,1)} %param.14) | copy-start | bytes 196612
  7.1 16.7 %copy-start.2 = (bf16[1,256,128]{2,1,0:T(8,128)(2,1)S(1)}, bf16[1,256,128]{2,1,0:T(8,128)(2,1)}, u32[]{:S(2)}) copy-start(bf16[1,256,128]{2,1,0:T(8,128)(2,1)} %param.15) | copy-start | bytes 196612
  7.1 16.7 %copy-start.3 = (bf16[1,256,128]{2,1,0:T(8,128)(2,1)S(1)}, bf16[1,256,128]{2,1,0:T(8,128)(2,1)}, u32[]{:S(2)}) copy-start(bf16[1,256,128]{2,1,0:T(8,128)(2,1)} %param.16) | copy-start | bytes 196612
  7.1 16.7 %copy-start.5 = (s32[256]{0:T(256)S(1)}, s32[256]{0:T(256)}, u32[]{:S(2)}) copy-start(s32[256]{0:T(256)} %param.13) | copy-start | bytes 3076
  25.4 30.2 %all-to-all-start.1 = ((bf16[4,264,128]{2,1,0:T(8,128)(2,1)}), bf16[4,264,128]{2,1,0:T(8,128)(2,1)S(1)}, u32[]{:S(2)}, u32[]{:S(2)}) async-start(bf16[4,264,128]{2,1,0:T(8,128)(2,1)} %get-tuple-element.40), calls=%async_computation.1 | async-start | bytes 540672 | tf_op jit(solution)/shard_map/all_to_all | solution.py:380
  34.5 11.3 %collective-permute-start.1 = (bf16[264,256]{1,0:T(8,128)(2,1)S(1)}, bf16[264,256]{1,0:T(8,128)(2,1)S(1)}, u32[]{:S(2)}, u32[]{:S(2)}) collective-permute-start(bf16[264,256]{1,0:T(8,128)(2,1)S(1)} %get-tuple-element.41.refs_1_), channel_id=1, source_target_pairs={{0,2},{1,3},{2,4},{3,5},{4,6},{5,7},{6,8},{7,9},{8,10},{9,11},{10,... | collective-permute-start | bytes 405512 | tf_op jit(solution)/shard_map/ppermute | solution.py:375
  36.4 11.3 %collective-permute-start.5 = (bf16[264,256]{1,0:T(8,128)(2,1)S(1)}, bf16[264,256]{1,0:T(8,128)(2,1)S(1)}, u32[]{:S(2)}, u32[]{:S(2)}) collective-permute-start(bf16[264,256]{1,0:T(8,128)(2,1)S(1)} %get-tuple-element.41.refs_1_), channel_id=1, source_target_pairs={{0,14},{1,15},{2,0},{3,1},{4,2},{5,3},{6,4},{7,5},{8,6},{9,7},{10,... | collective-permute-start | bytes 405512 | tf_op jit(solution)/shard_map/ppermute | solution.py:378
  45.8 7.9 %collective-permute-start.2 = (bf16[264,256]{1,0:T(8,128)(2,1)S(1)}, bf16[264,256]{1,0:T(8,128)(2,1)S(1)}, u32[]{:S(2)}, u32[]{:S(2)}) collective-permute-start(bf16[264,256]{1,0:T(8,128)(2,1)S(1)} %collective-permute-done.1.refs_2_), channel_id=1, source_target_pairs={{0,2},{1,3},{2,4},{3,5},{4,6},{5,7},{6,8},{7,9},{8,10},{9,11},{10,... | collective-permute-start | bytes 405512 | tf_op jit(solution)/shard_map/ppermute | solution.py:375
  47.7 9.9 %collective-permute-start.6 = (bf16[264,256]{1,0:T(8,128)(2,1)S(1)}, bf16[264,256]{1,0:T(8,128)(2,1)S(1)}, u32[]{:S(2)}, u32[]{:S(2)}) collective-permute-start(bf16[264,256]{1,0:T(8,128)(2,1)S(1)} %collective-permute-done.5.refs_3_), channel_id=1, source_target_pairs={{0,14},{1,15},{2,0},{3,1},{4,2},{5,3},{6,4},{7,5},{8,6},{9,7},{10,... | collective-permute-start | bytes 405512 | tf_op jit(solution)/shard_map/ppermute | solution.py:378
  53.7 9.4 %collective-permute-start.3 = (bf16[264,256]{1,0:T(8,128)(2,1)S(1)}, bf16[264,256]{1,0:T(8,128)(2,1)S(1)}, u32[]{:S(2)}, u32[]{:S(2)}) collective-permute-start(bf16[264,256]{1,0:T(8,128)(2,1)S(1)} %collective-permute-done.2.refs_1_), channel_id=1, source_target_pairs={{0,2},{1,3},{2,4},{3,5},{4,6},{5,7},{6,8},{7,9},{8,10},{9,11},{10,... | collective-permute-start | bytes 405512 | tf_op jit(solution)/shard_map/ppermute | solution.py:375
  57.6 8.9 %collective-permute-start.7 = (bf16[264,256]{1,0:T(8,128)(2,1)S(1)}, bf16[264,256]{1,0:T(8,128)(2,1)S(1)}, u32[]{:S(2)}, u32[]{:S(2)}) collective-permute-start(bf16[264,256]{1,0:T(8,128)(2,1)S(1)} %collective-permute-done.6.refs_2_), channel_id=1, source_target_pairs={{0,14},{1,15},{2,0},{3,1},{4,2},{5,3},{6,4},{7,5},{8,6},{9,7},{10,... | collective-permute-start | bytes 405512 | tf_op jit(solution)/shard_map/ppermute | solution.py:378
  63.1 7.9 %collective-permute-start.4 = (bf16[264,256]{1,0:T(8,128)(2,1)S(1)}, bf16[264,256]{1,0:T(8,128)(2,1)S(1)}, u32[]{:S(2)}, u32[]{:S(2)}) collective-permute-start(bf16[264,256]{1,0:T(8,128)(2,1)S(1)} %collective-permute-done.3.refs_1_), channel_id=1, source_target_pairs={{0,2},{1,3},{2,4},{3,5},{4,6},{5,7},{6,8},{7,9},{8,10},{9,11},{10,... | collective-permute-start | bytes 405512 | tf_op jit(solution)/shard_map/ppermute | solution.py:375
  71.0 17.9 %copy-start.4 = (bf16[1,128,256]{2,1,0:T(8,128)(2,1)S(1)}, bf16[1,128,256]{2,1,0:T(8,128)(2,1)}, u32[]{:S(2)}) copy-start(bf16[1,128,256]{2,1,0:T(8,128)(2,1)} %param.17) | copy-start | bytes 196612

commit v2 on v1

--- a/solution.py
+++ b/solution.py
@@ -35,18 +35,26 @@
     return lax.broadcasted_iota(jnp.int32, shape, dim)
 
 
-def row_to_column(row):
-    size = row.shape[1]
-    square = (size, size)
-    kept = jnp.where(iota(square, 0) == iota(square, 1), row, jnp.zeros_like(row))
-    return jnp.sum(kept, axis=1, keepdims=True)
+def row_to_column(row, width):
+    square = (width, width)
+    same = iota(square, 0) == iota(square, 1)
+    parts = []
+    for start in range(0, row.shape[1], width):
+        kept = jnp.where(same, row[:, start : start + width], 0.0)
+        parts.append(jnp.broadcast_to(jnp.sum(kept, axis=1, keepdims=True), square))
+    return jnp.concatenate(parts, axis=0)
 
 
 def column_to_row(column):
-    size = column.shape[0]
-    square = (size, size)
-    kept = jnp.where(iota(square, 0) == iota(square, 1), column, jnp.zeros_like(column))
-    return jnp.sum(kept, axis=0, keepdims=True)
+    width = column.shape[1]
+    square = (width, width)
+    same = iota(square, 0) == iota(square, 1)
+    return [
+        jnp.sum(
+            jnp.where(same, column[start : start + width, :], 0.0), axis=0, keepdims=True
+        )
+        for start in range(0, column.shape[0], width)
+    ]
 
 
 def fill_diagonal(weights, wide):
@@ -101,24 +109,34 @@
     signal,
     wide,
     receive,
-    query_weight,
     key_weight,
     value_weight,
     blocks,
     resid_out,
-    query_out,
     pair_out,
+    plain_out,
     source,
     spread,
 ):
     count, width = signal.shape
-    head = query_weight.shape[1]
+    head = key_weight.shape[1]
     source[...] = dot_tn(shuffled[...], receive[...])
     fill_taps(source, taps, count, spread)
     second = dot(spread[...], wide[...])
     resid = (signal[...].astype(F32) + second).astype(BF16)
     resid_out[...] = resid
-    queries = dot(resid, query_weight[...]).astype(BF16)
+    marks = blocks[...].astype(F32)
+    for start, weight in ((0, key_weight), (head, value_weight)):
+        projected = dot(resid, weight[...]).astype(BF16)
+        pair_out[:count, start : start + head] = projected
+        plain_out[:, start : start + head] = projected
+    pair_out[count:, :] = jnp.broadcast_to(marks, (EXTRA, width)).astype(BF16)
+
+
+def query_kernel(resid, query_weight, blocks, query_out):
+    count = resid.shape[0]
+    head = query_weight.shape[1]
+    queries = dot(resid[...], query_weight[...]).astype(BF16)
     marks = blocks[...].astype(F32)
     extra = jnp.concatenate(
         [
@@ -130,9 +148,6 @@
     for member in range(query_out.shape[0]):
         query_out[member, :count, :] = queries
         query_out[member, count:, :] = extra
-    pair_out[:count, :head] = dot(resid, key_weight[...]).astype(BF16)
-    pair_out[:count, head:] = dot(resid, value_weight[...]).astype(BF16)
-    pair_out[count:, :] = jnp.broadcast_to(marks, (EXTRA, width)).astype(BF16)
 
 
 def split_three(value):
@@ -144,10 +159,16 @@
     return pieces
 
 
-def attend_kernel(held, fresh, last, *refs):
+def attend_kernel(held, shifts, last, *refs):
+    fresh = len(shifts)
     query_ref, pairs = refs[0], refs[1 : 1 + fresh]
     old = refs[1 + fresh : 1 + fresh + held]
     outs = refs[1 + fresh + held :]
+    mine = lax.axis_index("tm")
+    length = lax.axis_size("tm") // 2
+    ring = length // 2
+    place = lax.rem(mine, length)
+    group, parity = place // 2, lax.rem(place, 2)
     members, count, head = query_ref.shape
     count = count - EXTRA
     half = EXTRA // 2
@@ -166,16 +187,25 @@
                 ],
                 axis=1,
             ).astype(F32)
-            marks = jnp.broadcast_to(row_to_column(marks), shape)
+            marks = row_to_column(marks, head)
             before = jnp.full(shape, FLOOR, F32)
         tiles = []
         most = before
-        for pair in pairs:
+        asker = (member // 2) * length + 2 * group + member % 2
+        for pair, shift in zip(pairs, shifts):
             scores = dot_nt(queries, pair[:count, :head])
+            if shift is not None:
+                holder = (
+                    (mine // length) * length + 2 * lax.rem(group - shift + ring, ring) + parity
+                )
+                hidden = jnp.where(holder < asker, jnp.float32(0.0), jnp.float32(NEG))
             for part in range(halves):
                 span = slice(part * head, (part + 1) * head)
-                seen = pair[count : count + 1, span].astype(F32) <= marks
-                masked = jnp.where(seen, scores[:, span], NEG)
+                if shift is None:
+                    seen = pair[count : count + 1, span].astype(F32) <= marks
+                    masked = jnp.where(seen, scores[:, span], NEG)
+                else:
+                    masked = scores[:, span] + hidden
                 most = jnp.maximum(most, masked)
                 tiles.append(masked)
         peak = jnp.broadcast_to(jnp.max(most, axis=1, keepdims=True), shape)
@@ -198,8 +228,8 @@
             outs[0][member, :count, :] = shared.astype(BF16)
             rows = []
             for column in (peak, total):
-                for piece in split_three(column_to_row(column[:, :1])):
-                    rows += [piece[:, :head], piece[:, head:]]
+                both = [split_three(row) for row in column_to_row(column)]
+                rows += [half[k] for k in range(3) for half in both]
             rows.append(jnp.zeros((STATS - len(rows), head), F32))
             outs[0][member, count:, :] = jnp.concatenate(rows, axis=0).astype(BF16)
 
@@ -238,7 +268,7 @@
     whole = functools.reduce(jnp.add, shares)
     summed = jnp.zeros((count, head), F32)
     for member in range(members):
-        share = row_to_column(shares[member] / whole)
+        share = row_to_column(shares[member] / whole, head)
         part = jnp.where(
             own_member() == member, own[...], parts[member, :count, :].astype(F32)
         )
@@ -326,19 +356,18 @@
         concat_axis=0,
         tiled=True,
     ).reshape(width, padded)
-    resid, queries, pair = call(
+    resid, pair, plain = call(
         functools.partial(second_kernel, taps),
         [
             pltpu.VMEM((count, width), BF16),
-            pltpu.VMEM((2 * rows, count + EXTRA, head), BF16),
             pltpu.VMEM((count + EXTRA, width), BF16),
+            pltpu.VMEM((count, width), BF16),
         ],
         (
             shuffled,
             signal,
             second_wide,
             receive,
-            query_weight.reshape(width, head),
             key_weight.reshape(width, head),
             value_weight.reshape(width, head),
             blocks.reshape(1, count),
@@ -362,29 +391,36 @@
         pltpu.VMEM((count, head), F32),
     ]
 
-    def attend(state, fresh, last=False):
+    def attend(state, fresh, step):
+        last = step == ring // 2
+        fresh, shifts = zip(*fresh)
         return call(
-            functools.partial(attend_kernel, len(state), len(fresh), last),
+            functools.partial(attend_kernel, len(state), shifts, last),
             last_shapes if last else state_shapes,
             (queries, *fresh, *state),
         )
 
-    state, fresh = (), [pair]
-    ahead = behind = pair
+    state, fresh = (), [(pair, None)]
+    ahead, behind = plain, pair
     for step in range(ring // 2):
         ahead = lax.ppermute(ahead, "tm", ring_shift(rows, length, 2))
         both = 2 * step + 2 < ring
         if both:
             behind = lax.ppermute(behind, "tm", ring_shift(rows, length, -2))
         if step == 0:
+            (queries,) = call(
+                query_kernel,
+                [pltpu.VMEM((2 * rows, count + EXTRA, head), BF16)],
+                (resid, query_weight.reshape(width, head), blocks.reshape(1, count)),
+            )
             queries = exchange(queries)
         else:
-            state = attend(state, fresh)
+            state = attend(state, fresh, step)
             fresh = []
             if step + 1 < ring // 2:
                 behind, *state = lax.optimization_barrier((behind, *state))
-        fresh = fresh + ([ahead, behind] if both else [ahead])
-    state = attend(state, fresh, last=True)
+        fresh = fresh + [(ahead, step + 1)] + ([(behind, None)] if both else [])
+    state = attend(state, fresh, ring // 2)
     parts = exchange(state[0])
     return pl.pallas_call(
         finish_kernel,

time: 90.4 us -> 89 us (0.985)
  the two profiles are of different devices: /device:TPU:1 before, /device:TPU:8 now
where the time goes in v2:
time: 89 us; the launch traced here: 88.4 us
  starting transfers between devices  33.9 us (38%)
  blocking collectives  23.9 us (27%)
  waiting for transfers between devices  17.5 us (20%)
  Pallas kernels  12.1 us (14%)
    ppermute x3, starting transfers between devices, per_device(): behind = lax.ppermute(behind, 'tm', ring_shift(rows, length, -2))  18.5 us
    all_to_all x1, blocking collectives, per_device(): lax.all_to_all(permuted.reshape(sources, width // sources, padded), 'freq...  14.9 us
    pallas_call x8, Pallas kernels, call(): pl.pallas_call(kernel, out_shape=outs, in_specs=[spec] * len(inputs), out...  11.1 us
    all_to_all x1, blocking collectives, per_device(): parts = exchange(state[0])  9.02 us
    ppermute x4, waiting for transfers between devices, per_device(): ahead = lax.ppermute(ahead, 'tm', ring_shift(rows, length, 2))  8.77 us
    ppermute x4, starting transfers between devices, per_device(): ahead = lax.ppermute(ahead, 'tm', ring_shift(rows, length, 2))  8.16 us
    ppermute x1, waiting for transfers between devices, per_device(): lax.ppermute(signal[count - 2 * margin:], 'tm', [(i, i + 1) for i in rang...  7.11 us
    ppermute x1, starting transfers between devices, per_device(): lax.ppermute(signal[count - 2 * margin:], 'tm', [(i, i + 1) for i in rang...  3.81 us
  transfers between devices with their start and end apart: 9, of which 6 were waited for; matrix products, arithmetic and copies ran while one was open for 0% of the time, Pallas kernels for 8%

profile of v2, /device:TPU:8, one launch (start us, length us, event | category | flops | bytes accessed | tf_op | source)
XLA Modules:
  0.0 88.4 jit_solution(1743301599901520122)
XLA Ops:
  0.0 0.8 slice.3
  0.8 3.8 %collective-permute-start = (bf16[16,256]{1,0:T(8,128)(2,1)S(1)}, bf16[16,256]{1,0:T(8,128)(2,1)S(1)}, u32[]{:S(2)}, u32[]{:S(2)}) collective-permute-start(bf16[16,256]{1,0:T(8,128)(2,1)S(1)} %slice.3), channel_id=1, source_target_pairs={{0,1},{1,2},{2,3},{3,4},{4,5},{5,6},{6,7},{7,8},{8,9},{9,10},{10,1... | collective-permute-start | bytes 24584 | tf_op jit(solution)/shard_map/ppermute | solution.py:329
  4.6 1.9 %shard_map.91 = (bf16[2304,256]{1,0:T(8,128)(2,1)S(1)}, bf16[2304,256]{1,0:T(8,128)(2,1)S(1)}, bf16[256,256]{1,0:T(8,128)(2,1)S(1)}, bf16[256,256]{1,0:T(8,128)(2,1)S(1)}) custom-call(bf16[4,9,64,64]{3,2,1,0:T(8,128)(2,1)} %first.1, bf16[4,9,64,64]{3,2,1,0:T(8,128)(2,1)} %second.1, s32[1,64]{1,0:T(1,128)} %bitcast.16), custom_call_target="tpu_custom_call" | custom-call | tf_op jit(solution)/shard_map/pallas_call | solution.py:286
  6.5 0.0 copy-start.1
  6.5 0.0 copy-start.2
  6.5 0.0 copy-start.5
  6.6 7.1 %collective-permute-done.before = bf16[16,256]{1,0:T(8,128)(2,1)S(1)} collective-permute-done((bf16[16,256]{1,0:T(8,128)(2,1)S(1)}, bf16[16,256]{1,0:T(8,128)(2,1)S(1)}, u32[]{:S(2)}, u32[]{:S(2)}) %collective-permute-start) | collective-permute-done | bytes 8224 | tf_op jit(solution)/shard_map/ppermute | solution.py:329
  13.7 0.8 shard_map.92
  14.5 0.0 copy-start.3
  14.5 14.9 %all_to_all.15 = bf16[16,16,264]{2,1,0:T(8,128)(2,1)S(1)} all-to-all(bf16[16,16,264]{2,1,0:T(8,128)(2,1)S(1)} %bitcast.9), channel_id=1, replica_groups=mesh['freq'=16,'tm'=32] {'freq'}, dimensions={0} | all-to-all | bytes 270336 | tf_op jit(solution)/shard_map/all_to_all | solution.py:352
  29.5 0.9 %shard_map.93 = (bf16[256,256]{1,0:T(8,128)(2,1)S(1)}, bf16[264,256]{1,0:T(8,128)(2,1)S(1)}, bf16[256,256]{1,0:T(8,128)(2,1)S(1)}) custom-call(bf16[256,264]{1,0:T(8,128)(2,1)S(1)} %bitcast.8, bf16[256,256]{1,0:T(8,128)(2,1)S(1)} %copy-done, bf16[2304,256]{1,0:T(8,128)(2,1)S(1)} %get-tuple-element.38.wide, bf16[256,256]{1,0:T(8,128)(2,1)S(1)} %get-tuple-element.39.receive, ...), custom_call_target="tpu_custom_call" | custom-call | tf_op jit(solution)/shard_map/pallas_call | solution.py:286
  30.4 0.9 shard_map.94
  31.3 3.4 %all-to-all-start.1 = ((bf16[4,264,128]{2,1,0:T(8,128)(2,1)}), bf16[4,264,128]{2,1,0:T(8,128)(2,1)S(1)}, u32[]{:S(2)}, u32[]{:S(2)}) async-start(bf16[4,264,128]{2,1,0:T(8,128)(2,1)} %shard_map.94), calls=%async_computation.1 | async-start | bytes 540672 | tf_op jit(solution)/shard_map/all_to_all | solution.py:416
  34.7 1.9 %collective-permute-start.1 = (bf16[256,256]{1,0:T(8,128)(2,1)S(1)}, bf16[256,256]{1,0:T(8,128)(2,1)S(1)}, u32[]{:S(2)}, u32[]{:S(2)}) collective-permute-start(bf16[256,256]{1,0:T(8,128)(2,1)S(1)} %get-tuple-element.41), channel_id=1, source_target_pairs={{0,2},{1,3},{2,4},{3,5},{4,6},{5,7},{6,8},{7,9},{8,10},{9,11},{10,... | collective-permute-start | bytes 393224 | tf_op jit(solution)/shard_map/ppermute | solution.py:406
  36.6 6.0 %collective-permute-start.5 = (bf16[264,256]{1,0:T(8,128)(2,1)S(1)}, bf16[264,256]{1,0:T(8,128)(2,1)S(1)}, u32[]{:S(2)}, u32[]{:S(2)}) collective-permute-start(bf16[264,256]{1,0:T(8,128)(2,1)S(1)} %get-tuple-element.42.refs_1_), channel_id=1, source_target_pairs={{0,14},{1,15},{2,0},{3,1},{4,2},{5,3},{6,4},{7,5},{8,6},{9,7},{10,... | collective-permute-start | bytes 405512 | tf_op jit(solution)/shard_map/ppermute | solution.py:409
  42.7 3.4 %collective-permute-done.1.refs_2_ = bf16[256,256]{1,0:T(8,128)(2,1)S(1)} collective-permute-done((bf16[256,256]{1,0:T(8,128)(2,1)S(1)}, bf16[256,256]{1,0:T(8,128)(2,1)S(1)}, u32[]{:S(2)}, u32[]{:S(2)}) %collective-permute-start.1) | collective-permute-done | bytes 131104 | tf_op jit(solution)/shard_map/ppermute | solution.py:406
  46.1 1.9 %collective-permute-start.2 = (bf16[256,256]{1,0:T(8,128)(2,1)S(1)}, bf16[256,256]{1,0:T(8,128)(2,1)S(1)}, u32[]{:S(2)}, u32[]{:S(2)}) collective-permute-start(bf16[256,256]{1,0:T(8,128)(2,1)S(1)} %collective-permute-done.1.refs_2_), channel_id=1, source_target_pairs={{0,2},{1,3},{2,4},{3,5},{4,6},{5,7},{6,8},{7,9},{8,10},{9,11},{10,... | collective-permute-start | bytes 393224 | tf_op jit(solution)/shard_map/ppermute | solution.py:406
  48.0 6.0 %collective-permute-start.6 = (bf16[264,256]{1,0:T(8,128)(2,1)S(1)}, bf16[264,256]{1,0:T(8,128)(2,1)S(1)}, u32[]{:S(2)}, u32[]{:S(2)}) collective-permute-start(bf16[264,256]{1,0:T(8,128)(2,1)S(1)} %collective-permute-done.5.refs_3_), channel_id=1, source_target_pairs={{0,14},{1,15},{2,0},{3,1},{4,2},{5,3},{6,4},{7,5},{8,6},{9,7},{10,... | collective-permute-start | bytes 405512 | tf_op jit(solution)/shard_map/ppermute | solution.py:409
  54.1 1.0 %collective-permute-done.2.refs_1_ = bf16[256,256]{1,0:T(8,128)(2,1)S(1)} collective-permute-done((bf16[256,256]{1,0:T(8,128)(2,1)S(1)}, bf16[256,256]{1,0:T(8,128)(2,1)S(1)}, u32[]{:S(2)}, u32[]{:S(2)}) %collective-permute-start.2) | collective-permute-done | bytes 131104 | tf_op jit(solution)/shard_map/ppermute | solution.py:406
  55.1 1.9 %collective-permute-start.3 = (bf16[256,256]{1,0:T(8,128)(2,1)S(1)}, bf16[256,256]{1,0:T(8,128)(2,1)S(1)}, u32[]{:S(2)}, u32[]{:S(2)}) collective-permute-start(bf16[256,256]{1,0:T(8,128)(2,1)S(1)} %collective-permute-done.2.refs_1_), channel_id=1, source_target_pairs={{0,2},{1,3},{2,4},{3,5},{4,6},{5,7},{6,8},{7,9},{8,10},{9,11},{10,... | collective-permute-start | bytes 393224 | tf_op jit(solution)/shard_map/ppermute | solution.py:406
  57.0 2.0 %shard_map.95 = (f32[4,256,128]{2,1,0:T(8,128)S(1)}, f32[4,256,128]{2,1,0:T(8,128)S(1)}, f32[4,256,128]{2,1,0:T(8,128)S(1)}, f32[4,256,128]{2,1,0:T(8,128)S(1)}) custom-call(bf16[4,264,128]{2,1,0:T(8,128)(2,1)S(1)} %all-to-all-done.1.refs_0_, bf16[264,256]{1,0:T(8,128)(2,1)S(1)} %get-tuple-element.42.refs_1_, ...), custom_call_target="tpu_custom_call" | custom-call | tf_op jit(solution)/shard_map/pallas_call | solution.py:286
  59.0 0.1 collective-permute-done.6.refs_2_
  59.1 6.5 %collective-permute-start.7 = (bf16[264,256]{1,0:T(8,128)(2,1)S(1)}, bf16[264,256]{1,0:T(8,128)(2,1)S(1)}, u32[]{:S(2)}, u32[]{:S(2)}) collective-permute-start(bf16[264,256]{1,0:T(8,128)(2,1)S(1)} %collective-permute-done.6.refs_2_), channel_id=1, source_target_pairs={{0,14},{1,15},{2,0},{3,1},{4,2},{5,3},{6,4},{7,5},{8,6},{9,7},{10,... | collective-permute-start | bytes 405512 | tf_op jit(solution)/shard_map/ppermute | solution.py:409
  65.6 0.0 collective-permute-done.3.refs_1_
  65.6 2.4 %collective-permute-start.4 = (bf16[256,256]{1,0:T(8,128)(2,1)S(1)}, bf16[256,256]{1,0:T(8,128)(2,1)S(1)}, u32[]{:S(2)}, u32[]{:S(2)}) collective-permute-start(bf16[256,256]{1,0:T(8,128)(2,1)S(1)} %collective-permute-done.3.refs_1_), channel_id=1, source_target_pairs={{0,2},{1,3},{2,4},{3,5},{4,6},{5,7},{6,8},{7,9},{8,10},{9,11},{10,... | collective-permute-start | bytes 393224 | tf_op jit(solution)/shard_map/ppermute | solution.py:406
  68.0 1.4 %shard_map.96 = (f32[4,256,128]{2,1,0:T(8,128)S(1)}, f32[4,256,128]{2,1,0:T(8,128)S(1)}, f32[4,256,128]{2,1,0:T(8,128)S(1)}, f32[4,256,128]{2,1,0:T(8,128)S(1)}) custom-call(bf16[4,264,128]{2,1,0:T(8,128)(2,1)S(1)} %all-to-all-done.1.refs_0_, bf16[256,256]{1,0:T(8,128)(2,1)S(1)} %collective-permute-done.2.refs_1_, ...), custom_call_target="tpu_custom_call" | custom-call | tf_op jit(solution)/shard_map/pallas_call | solution.py:286
  69.4 1.5 %collective-permute-done.7.refs_2_ = bf16[264,256]{1,0:T(8,128)(2,1)S(1)} collective-permute-done((bf16[264,256]{1,0:T(8,128)(2,1)S(1)}, bf16[264,256]{1,0:T(8,128)(2,1)S(1)}, u32[]{:S(2)}, u32[]{:S(2)}) %collective-permute-start.7) | collective-permute-done | bytes 135200 | tf_op jit(solution)/shard_map/ppermute | solution.py:409
  70.9 1.4 %shard_map.97 = (f32[4,256,128]{2,1,0:T(8,128)S(1)}, f32[4,256,128]{2,1,0:T(8,128)S(1)}, f32[4,256,128]{2,1,0:T(8,128)S(1)}, f32[4,256,128]{2,1,0:T(8,128)S(1)}) custom-call(bf16[4,264,128]{2,1,0:T(8,128)(2,1)S(1)} %all-to-all-done.1.refs_0_, bf16[256,256]{1,0:T(8,128)(2,1)S(1)} %collective-permute-done.3.refs_1_, ...), custom_call_target="tpu_custom_call" | custom-call | tf_op jit(solution)/shard_map/pallas_call | solution.py:286
  72.4 4.3 %collective-permute-done.4.refs_1_ = bf16[256,256]{1,0:T(8,128)(2,1)S(1)} collective-permute-done((bf16[256,256]{1,0:T(8,128)(2,1)S(1)}, bf16[256,256]{1,0:T(8,128)(2,1)S(1)}, u32[]{:S(2)}, u32[]{:S(2)}) %collective-permute-start.4) | collective-permute-done | bytes 131104 | tf_op jit(solution)/shard_map/ppermute | solution.py:406
  76.7 1.7 %shard_map.98 = (bf16[4,272,128]{2,1,0:T(8,128)(2,1)S(1)}, f32[256,128]{1,0:T(8,128)S(1)}) custom-call(bf16[4,264,128]{2,1,0:T(8,128)(2,1)S(1)} %all-to-all-done.1.refs_0_, bf16[256,256]{1,0:T(8,128)(2,1)S(1)} %collective-permute-done.4.refs_1_, f32[4,256,128]{2,1,0:T(8,128)S(1)} %get-tuple-element.61.refs_2_, f32[4,256,128]{2,1,0:T(8,128)S(1)} %get-tuple-element.62.refs_3_, ...), custom_call_target="tpu_custom_call" | custom-call | tf_op jit(solution)/shard_map/pallas_call | solution.py:286
  78.4 9.0 %all_to_all.16.parts = bf16[4,272,128]{2,1,0:T(8,128)(2,1)S(1)} all-to-all(bf16[4,272,128]{2,1,0:T(8,128)(2,1)S(1)} %get-tuple-element.65), channel_id=1, replica_groups={{0,1,16,17},{2,3,18,19},{4,5,20,21},{6,7,22,23},{8,9,24,25},{10,11,26,2..., dimensions={0} | all-to-all | bytes 557056 | tf_op jit(solution)/shard_map/all_to_all | solution.py:424
  87.4 1.0 %finish.1 = bf16[256,256]{1,0:T(8,128)(2,1)} custom-call(bf16[4,272,128]{2,1,0:T(8,128)(2,1)S(1)} %all_to_all.16.parts, f32[256,128]{1,0:T(8,128)S(1)} %get-tuple-element.66.own, bf16[256,256]{1,0:T(8,128)(2,1)S(1)} %get-tuple-element.40.resid, bf16[128,256]{1,0:T(8,128)(2,1)S(1)} %bitcast.13), custom_call_target="tpu_custom_call" | custom-call | tf_op jit(solution)/shard_map/finish/pallas_call | solution.py:425
  (10 shorter events, 0.0 us)
Async XLA Ops:
  0.0 13.7 %copy-start = (bf16[256,256]{1,0:T(8,128)(2,1)S(1)}, bf16[256,256]{1,0:T(8,128)(2,1)}, u32[]{:S(2)}) copy-start(bf16[256,256]{1,0:T(8,128)(2,1)} %signal.3) | copy-start | bytes 393220
  0.8 12.9 %collective-permute-start = (bf16[16,256]{1,0:T(8,128)(2,1)S(1)}, bf16[16,256]{1,0:T(8,128)(2,1)S(1)}, u32[]{:S(2)}, u32[]{:S(2)}) collective-permute-start(bf16[16,256]{1,0:T(8,128)(2,1)S(1)} %slice.3), channel_id=1, source_target_pairs={{0,1},{1,2},{2,3},{3,4},{4,5},{5,6},{6,7},{7,8},{8,9},{9,10},{10,1... | collective-permute-start | bytes 24584 | tf_op jit(solution)/shard_map/ppermute | solution.py:329
  6.5 22.9 %copy-start.1 = (bf16[1,256,128]{2,1,0:T(8,128)(2,1)S(1)}, bf16[1,256,128]{2,1,0:T(8,128)(2,1)}, u32[]{:S(2)}) copy-start(bf16[1,256,128]{2,1,0:T(8,128)(2,1)} %param.15) | copy-start | bytes 196612
  6.5 22.9 %copy-start.2 = (bf16[1,256,128]{2,1,0:T(8,128)(2,1)S(1)}, bf16[1,256,128]{2,1,0:T(8,128)(2,1)}, u32[]{:S(2)}) copy-start(bf16[1,256,128]{2,1,0:T(8,128)(2,1)} %param.16) | copy-start | bytes 196612
  6.5 22.9 %copy-start.5 = (s32[256]{0:T(256)S(1)}, s32[256]{0:T(256)}, u32[]{:S(2)}) copy-start(s32[256]{0:T(256)} %param.13) | copy-start | bytes 3076
  14.5 15.9 %copy-start.3 = (bf16[1,256,128]{2,1,0:T(8,128)(2,1)S(1)}, bf16[1,256,128]{2,1,0:T(8,128)(2,1)}, u32[]{:S(2)}) copy-start(bf16[1,256,128]{2,1,0:T(8,128)(2,1)} %param.14) | copy-start | bytes 196612
  31.3 25.8 %all-to-all-start.1 = ((bf16[4,264,128]{2,1,0:T(8,128)(2,1)}), bf16[4,264,128]{2,1,0:T(8,128)(2,1)S(1)}, u32[]{:S(2)}, u32[]{:S(2)}) async-start(bf16[4,264,128]{2,1,0:T(8,128)(2,1)} %shard_map.94), calls=%async_computation.1 | async-start | bytes 540672 | tf_op jit(solution)/shard_map/all_to_all | solution.py:416
  34.7 11.4 %collective-permute-start.1 = (bf16[256,256]{1,0:T(8,128)(2,1)S(1)}, bf16[256,256]{1,0:T(8,128)(2,1)S(1)}, u32[]{:S(2)}, u32[]{:S(2)}) collective-permute-start(bf16[256,256]{1,0:T(8,128)(2,1)S(1)} %get-tuple-element.41), channel_id=1, source_target_pairs={{0,2},{1,3},{2,4},{3,5},{4,6},{5,7},{6,8},{7,9},{8,10},{9,11},{10,... | collective-permute-start | bytes 393224 | tf_op jit(solution)/shard_map/ppermute | solution.py:406
  36.6 11.4 %collective-permute-start.5 = (bf16[264,256]{1,0:T(8,128)(2,1)S(1)}, bf16[264,256]{1,0:T(8,128)(2,1)S(1)}, u32[]{:S(2)}, u32[]{:S(2)}) collective-permute-start(bf16[264,256]{1,0:T(8,128)(2,1)S(1)} %get-tuple-element.42.refs_1_), channel_id=1, source_target_pairs={{0,14},{1,15},{2,0},{3,1},{4,2},{5,3},{6,4},{7,5},{8,6},{9,7},{10,... | collective-permute-start | bytes 405512 | tf_op jit(solution)/shard_map/ppermute | solution.py:409
  46.1 9.0 %collective-permute-start.2 = (bf16[256,256]{1,0:T(8,128)(2,1)S(1)}, bf16[256,256]{1,0:T(8,128)(2,1)S(1)}, u32[]{:S(2)}, u32[]{:S(2)}) collective-permute-start(bf16[256,256]{1,0:T(8,128)(2,1)S(1)} %collective-permute-done.1.refs_2_), channel_id=1, source_target_pairs={{0,2},{1,3},{2,4},{3,5},{4,6},{5,7},{6,8},{7,9},{8,10},{9,11},{10,... | collective-permute-start | bytes 393224 | tf_op jit(solution)/shard_map/ppermute | solution.py:406
  48.0 11.1 %collective-permute-start.6 = (bf16[264,256]{1,0:T(8,128)(2,1)S(1)}, bf16[264,256]{1,0:T(8,128)(2,1)S(1)}, u32[]{:S(2)}, u32[]{:S(2)}) collective-permute-start(bf16[264,256]{1,0:T(8,128)(2,1)S(1)} %collective-permute-done.5.refs_3_), channel_id=1, source_target_pairs={{0,14},{1,15},{2,0},{3,1},{4,2},{5,3},{6,4},{7,5},{8,6},{9,7},{10,... | collective-permute-start | bytes 405512 | tf_op jit(solution)/shard_map/ppermute | solution.py:409
  55.1 10.5 %collective-permute-start.3 = (bf16[256,256]{1,0:T(8,128)(2,1)S(1)}, bf16[256,256]{1,0:T(8,128)(2,1)S(1)}, u32[]{:S(2)}, u32[]{:S(2)}) collective-permute-start(bf16[256,256]{1,0:T(8,128)(2,1)S(1)} %collective-permute-done.2.refs_1_), channel_id=1, source_target_pairs={{0,2},{1,3},{2,4},{3,5},{4,6},{5,7},{6,8},{7,9},{8,10},{9,11},{10,... | collective-permute-start | bytes 393224 | tf_op jit(solution)/shard_map/ppermute | solution.py:406
  59.1 11.8 %collective-permute-start.7 = (bf16[264,256]{1,0:T(8,128)(2,1)S(1)}, bf16[264,256]{1,0:T(8,128)(2,1)S(1)}, u32[]{:S(2)}, u32[]{:S(2)}) collective-permute-start(bf16[264,256]{1,0:T(8,128)(2,1)S(1)} %collective-permute-done.6.refs_2_), channel_id=1, source_target_pairs={{0,14},{1,15},{2,0},{3,1},{4,2},{5,3},{6,4},{7,5},{8,6},{9,7},{10,... | collective-permute-start | bytes 405512 | tf_op jit(solution)/shard_map/ppermute | solution.py:409
  65.6 11.1 %collective-permute-start.4 = (bf16[256,256]{1,0:T(8,128)(2,1)S(1)}, bf16[256,256]{1,0:T(8,128)(2,1)S(1)}, u32[]{:S(2)}, u32[]{:S(2)}) collective-permute-start(bf16[256,256]{1,0:T(8,128)(2,1)S(1)} %collective-permute-done.3.refs_1_), channel_id=1, source_target_pairs={{0,2},{1,3},{2,4},{3,5},{4,6},{5,7},{6,8},{7,9},{8,10},{9,11},{10,... | collective-permute-start | bytes 393224 | tf_op jit(solution)/shard_map/ppermute | solution.py:406
  76.7 10.7 %copy-start.4 = (bf16[1,128,256]{2,1,0:T(8,128)(2,1)S(1)}, bf16[1,128,256]{2,1,0:T(8,128)(2,1)}, u32[]{:S(2)}) copy-start(bf16[1,128,256]{2,1,0:T(8,128)(2,1)} %param.17) | copy-start | bytes 196612
